TPU v7x, 256 devices: a whole 4x4x8 slice. The times are simulated.
256 devices in a mesh: group: 32 (over y, z), pencil: 8 (over x, core).
Axes of the slice: x: 4, y: 4, z: 8, core: 2. Of those that a mesh axis runs over, the one named last changes fastest.
Arguments:
- mult_iterate: float32 [32, 8, 8192], P('group', 'pencil'), may hold values from -6 to 6
- residual: float32 [32, 8, 8192], P('group', 'pencil'), may hold values from -6 to 6
- direction: float32 [32, 8, 8192], P('group', 'pencil'), may hold values from -6 to 6
- mult_scale: float32 [32, 8, 8192], P('group', 'pencil'), may hold values from 0.5 to 18
- eigen_basis: float32 [128, 3, 64, 64], P('group'), may hold values from -1 to 1
- eigen_values: float32 [128, 3, 64], P('group'), may hold values from 0.2 to 2
- elastic_coef: float32 [128, 3, 3], P('group'), may hold values from 0.5 to 2
- coarse_inverse: float32 [1024, 1024], replicated, may hold values from -1 to 2.5
- send_pos: int32 [32, 8, 16384], P('group', 'pencil'), may hold values from 0 to 24191, as said below
- pair_slots: int32 [32, 8, 2, 8192], P('group', 'pencil'), may hold values from 0 to 16383, as said below
- prim_rows: int32 [32, 8, 32], P('group', 'pencil'), may hold values from 0 to 16383, as said below
- coarse_idx: int32 [32, 8, 32], P('group', 'pencil'), may hold values from 0 to 1023
Outputs:
- new_iterate: float32 [32, 8, 8192], P('group', 'pencil')
- new_residual: float32 [32, 8, 8192], P('group', 'pencil')
- new_direction: float32 [32, 8, 8192], P('group', 'pencil')
Inputs may be any that keep to these rules, and one draw needn't show every extreme that they name: `send_pos`: distinct within each block (g, s). `pair_slots`: in each block (g, s) the two rows together hold every number of 0 to 16383 once. `prim_rows`: distinct within each block (g, s).
All inputs are finite; a program needn't handle non-finite values.
Results may differ from a plain program's by a relative error of at most 0.0003.
Values sent between devices are 32-bit elements; how exact they have to be, the bound alone decides.
No kernel may reach another device: no remote copies, remote signals or barrier semaphores. Data moves between devices by JAX's collectives and lax.ppermute only.
A program may use at most 128 MiB of HBM per device.

v0:
```python
import jax
import jax.numpy as jnp
from jax import lax
from jax.sharding import PartitionSpec as P


def cycle_slot(index, extent):
    cycle_size = 4 * extent - 4
    plane_index = index // cycle_size
    cycle_spot = index % cycle_size
    side_slot = jnp.where(
        cycle_spot < extent,
        cycle_spot,
        jnp.where(
            cycle_spot < 2 * extent - 2,
            cycle_spot + 1,
            jnp.where(cycle_spot < 3 * extent - 4, cycle_spot + 3, cycle_spot + 4),
        ),
    )
    return plane_index * 4 * extent + side_slot


def cycle_to_volume(cycles, extent):
    sides = cycles.reshape(cycles.shape[:-1] + (4, extent))
    count = jnp.arange(extent, dtype=jnp.int32)
    first_edge = (count == 0).astype(jnp.float32)
    last_edge = (count == extent - 1).astype(jnp.float32)
    plane = sides[..., 0, None, :] * first_edge[:, None]
    plane = plane + sides[..., 1, :, None] * first_edge[None, :]
    plane = plane + sides[..., 2, :, None] * last_edge[None, :]
    return plane + sides[..., 3, None, :] * last_edge[:, None]


def volume_to_cycle(volume):
    sides = jnp.stack(
        [volume[..., 0, :], volume[..., :, 0], volume[..., :, -1], volume[..., -1, :]], axis=-2
    )
    return sides.reshape(volume.shape[:-2] + (4 * volume.shape[-1],))


def spectrum(coeffs, along_x, along_y, along_z):
    first = coeffs[None, :, :, 0, None, None] * along_x.T[:, :, None, None, None]
    second = coeffs[None, :, :, 1, None, None] * along_y[None, :, None, :, None]
    third = coeffs[None, :, :, 2, None, None] * along_z[None, :, None, None, :]
    return first + second + third


def forward_yz(volume, basis):
    highest = lax.Precision.HIGHEST
    step_one = jnp.einsum("xpcyz,pzk->xpcyk", volume, basis[:, 2], precision=highest)
    return jnp.einsum("xpcyk,pyj->xpcjk", step_one, basis[:, 1], precision=highest)


def backward_yz(volume, basis):
    highest = lax.Precision.HIGHEST
    step_one = jnp.einsum("xpcjk,pyj->xpcyk", volume, basis[:, 1], precision=highest)
    return jnp.einsum("xpcyk,pzk->xpcyz", step_one, basis[:, 2], precision=highest)


def load_slab(arrived_rows, positions, slab_shape):
    cycle_total = slab_shape[0] * slab_shape[1] * slab_shape[2] * 4 * slab_shape[3]
    cycles = jnp.zeros((cycle_total,), jnp.float32).at[positions].set(arrived_rows)
    cycles = cycles.reshape(slab_shape[0], slab_shape[1], slab_shape[2], 4 * slab_shape[3])
    return cycle_to_volume(cycles, slab_shape[3])


def apply_inverse(arrived_rows, cycle_cells, basis, values, coeffs):
    highest = lax.Precision.HIGHEST
    pencils = lax.axis_size("pencil")
    extent = basis.shape[-1]
    patches = basis.shape[0]
    components = coeffs.shape[1]
    slab_x = extent // pencils
    slab_shape = (slab_x, patches, components, extent, extent)
    my_slab = lax.axis_index("pencil")
    row_start = my_slab * slab_x
    positions = cycle_slot(cycle_cells, extent)
    partial_yz = forward_yz(load_slab(arrived_rows, positions, slab_shape), basis)
    columns = lax.all_to_all(
        partial_yz.reshape(slab_x, patches, components, extent * extent),
        "pencil",
        split_axis=3,
        concat_axis=0,
        tiled=True,
    )
    columns = columns.reshape(extent, patches, components, slab_x, extent)
    spectral = jnp.einsum("xpcjk,pxi->ipcjk", columns, basis[:, 0], precision=highest)
    along_y = lax.dynamic_slice_in_dim(values[:, 1], row_start, slab_x, 1)
    scaled = spectral / spectrum(coeffs, values[:, 0], along_y, values[:, 2])
    mixed = jnp.einsum("ipcjk,pxi->xpcjk", scaled, basis[:, 0], precision=highest)
    mixed = mixed.reshape(extent, patches, components, slab_x * extent)
    back_x = lax.all_to_all(mixed, "pencil", split_axis=0, concat_axis=3, tiled=True).reshape(
        slab_shape
    )
    displace = backward_yz(back_x, basis)
    return volume_to_cycle(displace).reshape(-1)[positions]


def body(
    mult_iterate,
    residual,
    direction,
    mult_scale,
    eigen_basis,
    eigen_values,
    elastic_coef,
    coarse_inverse,
    send_pos,
    pair_slots,
    prim_rows,
    coarse_idx,
):
    highest = lax.Precision.HIGHEST
    groups = lax.axis_size("group")
    iterate_now = mult_iterate[0, 0]
    resid_now = residual[0, 0]
    search_dir = direction[0, 0]
    scale_now = mult_scale[0, 0]
    pair_rows = pair_slots[0, 0]
    cycle_cells = send_pos[0, 0]
    primal = prim_rows[0, 0]
    coarse_ids = coarse_idx[0, 0]
    rows_count = cycle_cells.shape[0]
    per_owner = rows_count // groups
    coarse_count = coarse_inverse.shape[0]
    old_part = jnp.sum(resid_now * scale_now * resid_now)
    old_norm = lax.psum(old_part, ("group", "pencil"))
    back_rows = (
        jnp.zeros((rows_count,), jnp.float32)
        .at[pair_rows[0]]
        .set(search_dir)
        .at[pair_rows[1]]
        .set(-search_dir)
    )
    arrived_rows = lax.all_to_all(
        back_rows.reshape(groups, per_owner), "group", split_axis=0, concat_axis=0, tiled=True
    ).reshape(rows_count)
    picked = apply_inverse(arrived_rows, cycle_cells, eigen_basis, eigen_values, elastic_coef)
    onehot = (coarse_ids[:, None] == jnp.arange(coarse_count, dtype=jnp.int32)[None, :]).astype(
        jnp.float32
    )
    local_coarse = jnp.dot(picked[primal], onehot, precision=highest)
    total_coarse = lax.psum(local_coarse, ("group", "pencil"))
    lifted = jnp.dot(coarse_inverse, total_coarse, precision=highest)
    sent_rows = picked.at[primal].add(jnp.dot(onehot, lifted, precision=highest))
    owner_rows = lax.all_to_all(
        sent_rows.reshape(groups, per_owner), "group", split_axis=0, concat_axis=0, tiled=True
    ).reshape(rows_count)
    mapped = owner_rows[pair_rows[0]] - owner_rows[pair_rows[1]]
    curvature = lax.psum(jnp.sum(search_dir * mapped), ("group", "pencil"))
    step_size = old_norm / curvature
    iterate_next = iterate_now + step_size * search_dir
    resid_next = resid_now - step_size * mapped
    precond = scale_now * resid_next
    norm_next = lax.psum(jnp.sum(resid_next * precond), ("group", "pencil"))
    search_next = precond + norm_next / old_norm * search_dir
    return (iterate_next[None, None], resid_next[None, None], search_next[None, None])


def solution(mesh):
    in_specs = (
        P("group", "pencil", None),
        P("group", "pencil", None),
        P("group", "pencil", None),
        P("group", "pencil", None),
        P("group", None, None, None),
        P("group", None, None),
        P("group", None, None),
        P(),
        P("group", "pencil", None),
        P("group", "pencil", None, None),
        P("group", "pencil", None),
        P("group", "pencil", None),
    )
    out_specs = (P("group", "pencil", None), P("group", "pencil", None), P("group", "pencil", None))
    return jax.shard_map(body, mesh=mesh, in_specs=in_specs, out_specs=out_specs, check_vma=False)
```

profile of v0, /device:TPU:1, one launch (start us, length us, event | category | flops | bytes accessed | tf_op | source)
XLA Modules:
  0.0 876.2 jit_solution(14388846261782737221)
XLA Ops:
  0.6 1.0 compare_select_fusion.4
  1.7 0.8 neg.3
  2.4 31.2 %scatter_custom_fusion = f32[16384]{0:T(1024)} fusion(s32[8192]{0:T(1024)S(1)} %bitcast.164, f32[8192]{0:T(1024)} %bitcast.154, f32[]{:T(128)} %constant.16.clone.1), kind=kCustom, calls=%fused_computation.81 | custom fusion | bytes 66048 | tf_op jit(solution)/shard_map/scatter | solution.py:131
  33.7 31.9 %scatter_fusion = f32[16384]{0:T(1024)} fusion(f32[16384]{0:T(1024)} %scatter_custom_fusion, s32[8192]{0:T(1024)S(1)} %bitcast.151, f32[8192]{0:T(1024)S(1)} %neg.3), kind=kCustom, calls=%fused_computation.5 | custom fusion | bytes 131072 | tf_op jit(solution)/shard_map/scatter | solution.py:133
  65.6 12.0 %all-to-all-start = ((f32[32,1,512]{2,1,0:T(1,128)}), f32[32,1,512]{2,1,0:T(1,128)S(1)}, u32[]{:S(2)}, u32[]{:S(2)}) async-start(f32[32,1,512]{2,1,0:T(1,128)} %bitcast.11), calls=%async_computation | async-start | bytes 131072 | tf_op jit(solution)/shard_map/all_to_all | solution.py:135
  77.6 0.8 compare_select_fusion
  78.5 8.0 all-to-all-done
  86.5 60.8 %scatter_custom_fusion.2 = f32[24576]{0:T(1024)S(1)} fusion(s32[16384]{0:T(1024)S(1)} %bitcast.160, f32[16384]{0:T(1024)S(1)} %bitcast.167, f32[]{:T(128)} %constant.16.clone.1), kind=kCustom, calls=%fused_computation.72 | custom fusion | bytes 98308 | tf_op jit(solution)/shard_map/scatter | solution.py:62
  147.7 4.0 fusion.8
  151.7 5.2 fusion.16
  156.9 34.6 %copy.135 = f32[8,4,3,64,64]{0,1,2,4,3:T(4,128)} copy(f32[8,4,3,64,64]{3,4,2,0,1:T(8,128)S(1)} %fusion.16) | data formatting | bytes 3145728 | tf_op jit(solution)/shard_map/reshape | solution.py:80
  191.5 31.9 %reshape.387 = f32[8,1,49152]{2,1,0:T(1,128)} reshape(f32[4096,3,4,8]{3,2,1,0:T(4,128)} %bitcast.146) | data formatting | bytes 3145728
  223.4 6.5 all-to-all-start.1
  230.6 0.7 broadcast_add_fusion
  231.3 19.2 %all-to-all-done.1 = f32[8,1,49152]{2,1,0:T(1,128)S(1)} async-done(((f32[8,1,49152]{2,1,0:T(1,128)}), f32[8,1,49152]{2,1,0:T(1,128)S(1)}, u32[]{:S(2)}, u32[]{:S(2)}) %all-to-all-start.1) | async-done | bytes 1572896 | tf_op jit(solution)/shard_map/all_to_all | solution.py:79
  251.0 4.4 reduce
  255.4 38.7 %reshape.388 = f32[4096,3,4,8]{3,2,1,0:T(4,128)} reshape(f32[8,49152]{1,0:T(8,128)S(1)} %reduce) | data formatting | bytes 3145728
  294.1 20.7 %copy.137 = f32[8,4,3,8,512]{4,0,3,2,1:T(8,128)} copy(f32[8,4,3,8,512]{0,1,2,4,3:T(4,128)} %bitcast.147) | data formatting | bytes 3145728 | tf_op jit(solution)/shard_map/all_to_all | solution.py:79
  314.8 2.6 reshape.305
  317.4 5.1 fusion.5
  322.5 3.2 fusion.2
  325.8 2.1 copy.119
  327.8 4.6 all-to-all-start.2
  332.5 0.6 broadcast_clamp_fusion.1
  333.1 0.6 broadcast_clamp_fusion
  333.7 19.3 %all-to-all-done.2 = f32[64,4,3,512]{3,1,2,0:T(4,128)S(1)} async-done(((f32[64,4,3,512]{3,1,2,0:T(4,128)}), f32[64,4,3,512]{3,1,2,0:T(4,128)S(1)}, u32[]{:S(2)}, u32[]{:S(2)}) %all-to-all-start.2) | async-done | bytes 1572896 | tf_op jit(solution)/shard_map/all_to_all | solution.py:92
  353.5 2.1 copy.140
  355.6 2.6 reshape.382
  358.3 5.1 fusion.35
  363.4 5.1 fusion.19
  368.5 2.7 fusion.58
  371.3 2.5 copy.124
  373.9 1.5 copy.125
  375.9 160.4 %gather_fusion = f32[16384]{0:T(1024)} fusion(f32[24576]{0:T(1024)S(1)} %reshape_reshape.7, s32[16384]{0:T(1024)S(1)} %copy-done.8), kind=kCustom, calls=%fused_computation | custom fusion | bytes 196608 | tf_op jit(solution)/shard_map/gather | solution.py:96
  536.3 1.6 gather_fusion.1
  538.1 72.8 %psum.29 = f32[1024]{0:T(1024)S(1)} all-reduce(f32[1024]{0:T(1024)S(1)} %bitcast.172), channel_id=1, replica_groups=mesh['group'=32,'pencil'=8] {'group','pencil'}, use_global_device_ids=true, to_apply=%region_5.6 | all-reduce | flops 1024 | bytes 8192 | tf_op jit(solution)/shard_map/psum | solution.py:143
  610.9 5.6 convolution_bitcast_fusion
  616.8 2.2 scatter_fusion.1
  619.0 5.0 all-to-all-start.3
  624.1 0.6 fusion.51
  624.7 8.2 all-to-all-done.3
  632.9 45.5 %gather_fusion.3 = f32[8192]{0:T(1024)S(1)} fusion(f32[16384]{0:T(1024)S(1)} %bitcast.144, s32[8192]{0:T(1024)S(1)} %copy-done.11), kind=kCustom, calls=%fused_computation.3 | custom fusion | bytes 98304 | tf_op jit(solution)/shard_map/gather | solution.py:149
  678.5 45.5 %gather_fusion.2 = f32[8192]{0:T(1024)S(1)} fusion(f32[16384]{0:T(1024)S(1)} %bitcast.145, s32[8192]{0:T(1024)S(1)} %broadcast_clamp_fusion.2), kind=kCustom, calls=%fused_computation.2 | custom fusion | bytes 98304 | tf_op jit(solution)/shard_map/gather | solution.py:149
  724.0 0.6 multiply_reduce_fusion
  724.6 73.3 %all-reduce = (f32[]{:T(128)}, f32[]{:T(128)}) all-reduce(f32[]{:T(128)} %fusion.51, f32[]{:T(128)} %get-tuple-element.9), channel_id=1, replica_groups=mesh['group'=32,'pencil'=8] {'group','pencil'}, use_global_device_ids=true, to_apply=%region_1.0 | all-reduce | flops 2 | bytes 16 | tf_op jit(solution)/shard_map/psum | solution.py:127
  799.3 0.6 fusion.52
  799.9 74.0 %psum.31 = f32[]{:T(128)} all-reduce(f32[]{:T(128)} %get-tuple-element.7), channel_id=1, replica_groups=mesh['group'=32,'pencil'=8] {'group','pencil'}, use_global_device_ids=true, to_apply=%region_10.11 | all-reduce | flops 1 | bytes 8 | tf_op jit(solution)/shard_map/psum | solution.py:155
  875.3 0.7 multiply_add_fusion
  (69 shorter events, 3.2 us)
Async XLA Ops:
  1.6 64.0 %copy-start.1 = (s32[8192,1]{0,1:T(1,128)}, s32[8192,1]{0,1:T(1,128)S(1)}, u32[]{:S(2)}) copy-start(s32[8192,1]{0,1:T(1,128)S(1)} %get-tuple-element.19) | copy-start | bytes 98308
  1.6 63.9 %copy-start.9 = (s32[8192,1]{0,1:T(1,128)}, s32[8192,1]{0,1:T(1,128)S(1)}, u32[]{:S(2)}) copy-start(s32[8192,1]{0,1:T(1,128)S(1)} %get-tuple-element.20) | copy-start | bytes 98308
  33.7 44.0 %copy-start.12 = (s32[1,1,16384]{2,1,0:T(1,128)S(1)}, s32[1,1,16384]{2,1,0:T(1,128)}, u32[]{:S(2)}) copy-start(s32[1,1,16384]{2,1,0:T(1,128)} %param.20) | copy-start | bytes 196612
  33.7 114.0 %copy-start = (f32[4,3,64,64]{3,2,1,0:T(8,128)S(1)}, f32[4,3,64,64]{3,2,1,0:T(8,128)}, u32[]{:S(2)}) copy-start(f32[4,3,64,64]{3,2,1,0:T(8,128)} %param.16) | copy-start | bytes 589828
  65.6 20.9 %all-to-all-start = ((f32[32,1,512]{2,1,0:T(1,128)}), f32[32,1,512]{2,1,0:T(1,128)S(1)}, u32[]{:S(2)}, u32[]{:S(2)}) async-start(f32[32,1,512]{2,1,0:T(1,128)} %bitcast.11), calls=%async_computation | async-start | bytes 131072 | tf_op jit(solution)/shard_map/all_to_all | solution.py:135
  78.4 8.1 copy-start.6
  223.4 6.5 copy-start.13
  223.4 7.0 copy-start.16
  223.4 27.1 %all-to-all-start.1 = ((f32[8,1,49152]{2,1,0:T(1,128)}), f32[8,1,49152]{2,1,0:T(1,128)S(1)}, u32[]{:S(2)}, u32[]{:S(2)}) async-start(f32[8,1,49152]{2,1,0:T(1,128)} %reshape.387), calls=%async_computation.1 | async-start | bytes 3145728 | tf_op jit(solution)/shard_map/all_to_all | solution.py:79
  317.4 5.1 copy-start.14
  325.8 6.7 copy-start.17
  327.8 4.6 copy-start.2
  327.8 5.2 copy-start.7
  327.8 25.2 %all-to-all-start.2 = ((f32[64,4,3,512]{3,1,2,0:T(4,128)}), f32[64,4,3,512]{3,1,2,0:T(4,128)S(1)}, u32[]{:S(2)}, u32[]{:S(2)}) async-start(f32[64,4,3,512]{3,1,2,0:T(4,128)} %copy.119), calls=%async_computation.2 | async-start | bytes 3145728 | tf_op jit(solution)/shard_map/all_to_all | solution.py:92
  371.3 4.6 copy-start.8
  375.9 162.0 %copy-start.18 = (s32[1,1,32]{2,1,0:T(1,128)S(1)}, s32[1,1,32]{2,1,0:T(1,128)}, u32[]{:S(2)}) copy-start(s32[1,1,32]{2,1,0:T(1,128)} %param.23) | copy-start | bytes 388
  536.3 87.7 %copy-start.10 = (s32[8192,1]{0,1:T(1,128)S(1)}, s32[8192,1]{0,1:T(1,128)}, u32[]{:S(2)}) copy-start(s32[8192,1]{0,1:T(1,128)} %copy-done.9) | copy-start | bytes 98308
  536.3 87.7 %copy-start.4 = (f32[1,1,8192]{2,1,0:T(1,128)S(1)}, f32[1,1,8192]{2,1,0:T(1,128)}, u32[]{:S(2)}) copy-start(f32[1,1,8192]{2,1,0:T(1,128)} %param.15) | copy-start | bytes 98308
  536.3 87.7 %copy-start.5 = (f32[1,1,8192]{2,1,0:T(1,128)S(1)}, f32[1,1,8192]{2,1,0:T(1,128)}, u32[]{:S(2)}) copy-start(f32[1,1,8192]{2,1,0:T(1,128)} %param.13) | copy-start | bytes 98308
  536.3 96.6 %copy-start.11 = (s32[8192]{0:T(1024)S(1)}, s32[8192]{0:T(1024)}, u32[]{:S(2)}) copy-start(s32[8192]{0:T(1024)} %broadcast_clamp_fusion.1) | copy-start | bytes 98308
  619.0 13.9 %all-to-all-start.3 = ((f32[32,1,512]{2,1,0:T(1,128)}), f32[32,1,512]{2,1,0:T(1,128)S(1)}, u32[]{:S(2)}, u32[]{:S(2)}) async-start(f32[32,1,512]{2,1,0:T(1,128)} %bitcast.57), calls=%async_computation.3 | async-start | bytes 131072 | tf_op jit(solution)/shard_map/all_to_all | solution.py:146
  678.4 45.6 %copy-start.3 = (f32[1,1,8192]{2,1,0:T(1,128)S(1)}, f32[1,1,8192]{2,1,0:T(1,128)}, u32[]{:S(2)}) copy-start(f32[1,1,8192]{2,1,0:T(1,128)} %param.14) | copy-start | bytes 98308
  678.4 196.8 %copy-start.15 = (f32[1,1,8192]{2,1,0:T(1,128)S(1)}, f32[1,1,8192]{2,1,0:T(1,128)}, u32[]{:S(2)}) copy-start(f32[1,1,8192]{2,1,0:T(1,128)} %param.12) | copy-start | bytes 98308
where the time goes:
time: 881 us; the launch traced here: 876 us
  local copies, waits for them, and re-layouts  521 us (59%)
  blocking collectives  220 us (25%)
  waiting for transfers between devices  54.7 us (6%)
  matrix products  33.9 us (4%)
  starting transfers between devices  28.2 us (3%)
  other arithmetic  14.1 us (2%)
    gather x1, local copies, waits for them, and re-layouts, apply_inverse(): return volume_to_cycle(displace).reshape(-1)[positions]  160 us
    gather x2, local copies, waits for them, and re-layouts, body(): mapped = owner_rows[pair_rows[0]] - owner_rows[pair_rows[1]]  91.1 us
    psum x1, blocking collectives, body(): norm_next = lax.psum(jnp.sum(resid_next * precond), ('group', 'pencil'))  74 us
    psum x1, blocking collectives, body(): old_norm = lax.psum(old_part, ('group', 'pencil'))  73.3 us
    psum x1, blocking collectives, body(): total_coarse = lax.psum(local_coarse, ('group', 'pencil'))  72.8 us
    unnamed x40, local copies, waits for them, and re-layouts  70.6 us
    scatter x2, local copies, waits for them, and re-layouts, body(): back_rows = jnp.zeros((rows_count,), jnp.float32).at[pair_rows[0]].set(se...  63.2 us
    scatter x1, local copies, waits for them, and re-layouts, load_slab(): jnp.zeros((cycle_total,), jnp.float32).at[positions].set(arrived_rows)  60.8 us
  transfers between devices with their start and end apart: 4, of which 4 were waited for; matrix products, arithmetic and copies ran while one was open for 0% of the time, Pallas kernels for 0%

commit v1 on v0

v1 whole, which is shorter than its diff:
```python
import functools

import jax
import jax.numpy as jnp
from jax import lax
from jax.experimental import pallas as pl
from jax.experimental.pallas import tpu as pltpu
from jax.sharding import PartitionSpec as P

LANES = 128
BF16 = jnp.bfloat16
F32 = jnp.float32
HIGHEST = lax.Precision.HIGHEST
VMEM = pl.BlockSpec(memory_space=pltpu.VMEM)


def call(kernel, out_shape, count, name, scratch=(), flops=1_000_000):
    single = not isinstance(out_shape, (tuple, list))
    return pl.pallas_call(
        kernel,
        out_shape=out_shape,
        in_specs=[VMEM] * count,
        out_specs=VMEM if single else [VMEM] * len(out_shape),
        scratch_shapes=list(scratch),
        name=name,
        cost_estimate=pl.CostEstimate(flops=flops, bytes_accessed=1 << 18, transcendentals=0),
    )


def split_channels(value, count):
    pieces = []
    for _ in range(count):
        piece = value.astype(BF16).astype(F32)
        pieces.append(piece)
        value = value - piece
    return pieces


def scatter_rows(rows, high_row, low_row, piece_rows, chunk, total, channels):
    row_ids = lax.broadcasted_iota(jnp.int32, (rows, LANES), 0).astype(F32).astype(BF16)
    lane_ids = lax.broadcasted_iota(jnp.int32, (LANES, LANES), 0).astype(F32).astype(BF16)

    def step(index, acc):
        left, right = [], []
        for r in range(chunk):
            high = jnp.broadcast_to(high_row(index, r), (rows, LANES)).astype(BF16)
            low = jnp.broadcast_to(low_row(index, r), (LANES, LANES)).astype(BF16)
            left.append(jnp.where(row_ids == high, BF16(1), BF16(0)))
            match = lane_ids == low
            right.append(
                jnp.concatenate(
                    [
                        jnp.where(
                            match,
                            jnp.broadcast_to(piece_rows(c, index, r), (LANES, LANES)).astype(BF16),
                            BF16(0),
                        )
                        for c in range(channels)
                    ],
                    axis=0,
                )
            )
        left = jnp.concatenate(left, axis=1)
        right = jnp.concatenate(right, axis=1)
        return acc + lax.dot_general(
            left, right, (((1,), (1,)), ((), ())), preferred_element_type=F32
        )

    acc = jnp.zeros((rows, LANES * channels), F32)
    if total == chunk:
        acc = step(0, acc)
    else:
        acc = lax.fori_loop(0, total // chunk, step, acc)
    out = acc[:, :LANES]
    for c in range(1, channels):
        out = out + acc[:, c * LANES : (c + 1) * LANES]
    return out


def gather_block(indices, table_row, table_rows, chains=4):
    high = lax.shift_right_arithmetic(indices, 7)
    low = jnp.bitwise_and(indices, LANES - 1)
    acc = [jnp.zeros(indices.shape, F32) for _ in range(chains)]
    for a in range(table_rows):
        row = jnp.broadcast_to(table_row(a), indices.shape)
        picked = jnp.take_along_axis(row, low, axis=1, mode="promise_in_bounds")
        acc[a % chains] = jnp.where(high == a, picked, acc[a % chains])
    out = acc[0]
    for other in acc[1:]:
        out = out + other
    return out


def split_index(idx_ref, high_ref, low_ref):
    idx = idx_ref[...]
    high_ref[...] = lax.shift_right_arithmetic(idx, 7).astype(F32)
    low_ref[...] = jnp.bitwise_and(idx, LANES - 1).astype(F32)


CHUNK = 16


def back_kernel(idx_ref, dir_ref, extra_ref, out_ref, high_ref, low_ref, piece_ref, acc_ref):
    split_index(idx_ref, high_ref, low_ref)
    half = dir_ref.shape[0]
    for c, piece in enumerate(split_channels(dir_ref[...], 2)):
        piece_ref[c, :half, :] = piece
        piece_ref[c, half:, :] = -piece
    rows = idx_ref.shape[0]
    acc_ref[...] = scatter_rows(
        rows,
        lambda t, r: high_ref[pl.ds(t * CHUNK + r, 1), :],
        lambda t, r: low_ref[pl.ds(t * CHUNK + r, 1), :],
        lambda c, t, r: piece_ref[c, pl.ds(t * CHUNK + r, 1), :],
        CHUNK,
        rows,
        2,
    )
    for h in range(out_ref.shape[0]):
        out_ref[h, 0:4, :] = acc_ref[4 * h : 4 * h + 4, :]
        out_ref[h, 4:8, :] = extra_ref[0:4, :]


def load_kernel(arr_ref, idx_ref, out_ref, high_ref, low_ref, piece_ref, acc_ref):
    split_index(idx_ref, high_ref, low_ref)
    rows = idx_ref.shape[0]
    groups = arr_ref.shape[0]
    values = arr_ref[...].reshape(groups * 8, LANES)
    for c, piece in enumerate(split_channels(values, 2)):
        piece_ref[c] = piece
    table = acc_ref.shape[0]
    acc_ref[...] = scatter_rows(
        table,
        lambda t, r: high_ref[pl.ds(t * CHUNK + r, 1), :],
        lambda t, r: low_ref[pl.ds(t * CHUNK + r, 1), :],
        lambda c, t, r: piece_ref[c, pl.ds(t * CHUNK * 2 + (r // 4) * 8 + r % 4, 1), :],
        CHUNK,
        rows,
        2,
    )
    for dest in range(out_ref.shape[0]):
        for half in range(2):
            start = (dest // 2) * 48 + half * 24
            out_ref[dest, :, half * LANES : (half + 1) * LANES] = acc_ref[start : start + 24, :]


def full_dot(left, right, contract):
    return lax.dot_general(
        left, right, ((contract[0], contract[1]), ((), ())), precision=HIGHEST,
        preferred_element_type=F32,
    )


def solve_kernel(
    recv_ref, bxt_ref, bx_ref, bdt_ref, bd_ref, cst_ref, out_ref, fwd_ref, d0_ref, d1_ref
):
    sources = recv_ref.shape[0]
    load = jnp.concatenate(
        [recv_ref[src, 8 * c : 8 * c + 8, :] for c in range(3) for src in range(sources)], axis=0
    )
    along_x = full_dot(bxt_ref[...], load, ((1,), (0,)))
    fwd_ref[...] = full_dot(bdt_ref[...], along_x, ((1,), (1,)))

    def step(j, carry):
        top, bottom = carry

        def row(index):
            return jnp.broadcast_to(cst_ref[index, pl.ds(j, 1), :], (64, LANES))

        first = jnp.broadcast_to(fwd_ref[pl.ds(64 + j, 1), :], (64, LANES))
        last = jnp.broadcast_to(fwd_ref[pl.ds(128 + j, 1), :], (64, LANES))
        y_first, y_last = row(0), row(1)
        spectral = (
            y_first * fwd_ref[0:64, :]
            + y_last * fwd_ref[192:256, :]
            + first * cst_ref[2]
            + last * cst_ref[3]
        )
        scaled = spectral / (row(4) + cst_ref[5])
        along_first = cst_ref[2] * scaled
        along_last = cst_ref[3] * scaled
        d0_ref[j] = jnp.sum(along_first.reshape(8, 8, LANES), axis=0)
        d1_ref[j] = jnp.sum(along_last.reshape(8, 8, LANES), axis=0)
        return top + y_first * scaled, bottom + y_last * scaled

    zero = jnp.zeros((64, LANES), F32)
    top, bottom = lax.fori_loop(0, 64, step, (zero, zero), unroll=4)
    edges = jnp.concatenate(
        [top, jnp.sum(d0_ref[...], axis=1), jnp.sum(d1_ref[...], axis=1), bottom], axis=0
    )
    cells = full_dot(bd_ref[...], edges, ((1,), (0,)))
    slabs = full_dot(bx_ref[...], cells, ((1,), (1,)))
    for c in range(3):
        for dest in range(out_ref.shape[0]):
            out_ref[dest, 8 * c : 8 * c + 8, :] = slabs[
                64 * c + 8 * dest : 64 * c + 8 * dest + 8, :
            ]


def pick_kernel(recv_ref, idx_ref, out_ref, table_ref, pick_ref):
    for p in range(recv_ref.shape[0] // 2):
        for half in range(2):
            lanes = slice(half * LANES, (half + 1) * LANES)
            start = p * 48 + half * 24
            table_ref[start : start + 24, :] = (
                recv_ref[2 * p, :, lanes] + recv_ref[2 * p + 1, :, lanes]
            )
    table_rows = table_ref.shape[0]

    def table_row(a):
        return table_ref[a : a + 1, :]

    def block(t, carry):
        start = pl.multiple_of(t * 16, 16)
        pick_ref[pl.ds(start, 16), :] = gather_block(
            idx_ref[pl.ds(start, 16), :], table_row, table_rows, 2
        )
        return carry

    lax.fori_loop(0, 9, block, 0)
    primal = pick_ref[128:132, :]
    for h in range(out_ref.shape[0]):
        out_ref[h, 0:4, :] = pick_ref[4 * h : 4 * h + 4, :]
        out_ref[h, 4:8, :] = primal


def coarse_kernel(arr_ref, ids_ref, out_ref, high_ref, low_ref, piece_ref):
    split_index(ids_ref, high_ref, low_ref)
    packed = []
    for q in range(8):
        row = arr_ref[4 * q, 4:5, :]
        for step in range(1, 4):
            row = row + arr_ref[4 * q + step, 4:5, :]
        packed.append(row)
    for c, piece in enumerate(split_channels(jnp.concatenate(packed, axis=0), 3)):
        piece_ref[c] = piece
    partial = scatter_rows(
        16,
        lambda t, r: high_ref[pl.ds(r, 1), :],
        lambda t, r: low_ref[pl.ds(r, 1), :],
        lambda c, t, r: piece_ref[c, pl.ds(r, 1), :],
        8,
        8,
        3,
    )
    for dest in range(out_ref.shape[0]):
        out_ref[dest] = partial[0:8, :]


def image_kernel(
    coarse_ref, inv_ref, ids_ref, place_ref, arr_ref, pair_ref, dir_ref, res_ref, scale_ref,
    image_ref, sums_ref, mid_ref, prod_ref, high_ref, low_ref, piece_ref, table_ref,
):
    total = coarse_ref[0]
    for src in range(1, coarse_ref.shape[0]):
        total = total + coarse_ref[src]
    mid_ref[...] = total
    coarse_rows = [jnp.broadcast_to(mid_ref[q : q + 1, :], (LANES, LANES)) for q in range(8)]

    ids = ids_ref[...]
    ids_high = lax.shift_right_arithmetic(ids, 7)
    ids_low = jnp.bitwise_and(ids, LANES - 1)
    ones = jnp.ones((8, LANES), F32)
    lifted = jnp.zeros((8, LANES), F32)
    for block in range(8):
        rows = slice(block * LANES, (block + 1) * LANES)
        product = inv_ref[rows, 0:LANES] * coarse_rows[0]
        for q in range(1, 8):
            product = product + inv_ref[rows, q * LANES : (q + 1) * LANES] * coarse_rows[q]
        prod_ref[...] = product
        lifted_row = full_dot(ones, prod_ref[...], ((1,), (1,)))
        picked = jnp.take_along_axis(lifted_row, ids_low, axis=1, mode="promise_in_bounds")
        lifted = jnp.where(ids_high == block, picked, lifted)

    split_index(place_ref, high_ref, low_ref)
    for c, piece in enumerate(split_channels(lifted, 3)):
        piece_ref[c] = piece
    rows = table_ref.shape[0]
    table_ref[...] = arr_ref[...].reshape(rows, LANES) + scatter_rows(
        rows,
        lambda t, r: high_ref[pl.ds(r, 1), :],
        lambda t, r: low_ref[pl.ds(r, 1), :],
        lambda c, t, r: piece_ref[c, pl.ds(r, 1), :],
        8,
        8,
        3,
    )

    def table_row(a):
        row = (a // 4) * 8 + a % 4
        return table_ref[row : row + 1, :]

    half = dir_ref.shape[0]

    def block(t, sums):
        start = pl.multiple_of(t * 8, 8)
        both = jnp.concatenate(
            [pair_ref[pl.ds(start, 8), :], pair_ref[pl.ds(half + start, 8), :]], axis=0
        )
        picked = gather_block(both, table_row, rows // 2, 2)
        image = picked[0:8] - picked[8:16]
        image_ref[pl.ds(start, 8), :] = image
        res = res_ref[pl.ds(start, 8), :]
        scaled = scale_ref[pl.ds(start, 8), :]
        scaled_res = res * scaled
        return (
            sums[0] + scaled_res * res,
            sums[1] + dir_ref[pl.ds(start, 8), :] * image,
            sums[2] + scaled_res * image,
            sums[3] + (scaled * image) * image,
        )

    zero = jnp.zeros((8, LANES), F32)
    sums = lax.fori_loop(0, half // 8, block, (zero, zero, zero, zero))
    lane = lax.broadcasted_iota(jnp.int32, (8, LANES), 1)
    packed = jnp.zeros((8, LANES), F32)
    for n, part in enumerate(sums):
        value = jnp.sum(jnp.sum(part, axis=0, keepdims=True), axis=1, keepdims=True)
        packed = jnp.where(lane == n, jnp.broadcast_to(value, (8, LANES)), packed)
    for t in range(sums_ref.shape[0] // 8):
        sums_ref[8 * t : 8 * t + 8, :] = packed


def update_kernel(
    sums_ref, iterate_ref, res_ref, dir_ref, scale_ref, image_ref, it_out, res_out, dir_out
):
    totals = jnp.sum(sums_ref[...], axis=0, keepdims=True)
    lane = lax.broadcasted_iota(jnp.int32, (1, LANES), 1)

    def pick(n):
        return jnp.sum(jnp.where(lane == n, totals, 0.0), axis=1, keepdims=True)

    old, curvature, cross, square = pick(0), pick(1), pick(2), pick(3)
    alpha = old / curvature
    new = old - 2.0 * alpha * cross + (alpha * alpha) * square
    beta = new / old
    direction = dir_ref[...]
    res_next = res_ref[...] - alpha * image_ref[...]
    it_out[...] = iterate_ref[...] + alpha * direction
    res_out[...] = res_next
    dir_out[...] = scale_ref[...] * res_next + beta * direction


def slot_index(cells):
    plane = cells // 252
    spot = cells % 252
    slot = (
        spot
        + (spot >= 64).astype(jnp.int32)
        + 2 * (spot >= 126).astype(jnp.int32)
        + (spot >= 188).astype(jnp.int32)
    )
    along_x = plane // 12
    patch = (plane % 12) // 3
    component = plane % 3
    row = patch * 48 + (slot // LANES) * 24 + component * 8 + along_x
    return row * LANES + slot % LANES


def exchange(array, axis):
    return lax.all_to_all(array, axis, split_axis=0, concat_axis=0, tiled=True)


def solve_constants(basis, values, coeffs, pencil):
    patch, half = pencil // 2, pencil % 2
    own = lax.dynamic_index_in_dim(basis, patch, 0, keepdims=False)
    own_values = lax.dynamic_index_in_dim(values, patch, 0, keepdims=False)
    own_coeffs = lax.dynamic_index_in_dim(coeffs, patch, 0, keepdims=False)
    half_x = lax.dynamic_slice(own[0], (0, half * 32), (64, 32))
    rows = jnp.arange(192, dtype=jnp.int32)[:, None] // 64
    lanes = jnp.arange(LANES, dtype=jnp.int32)[None, :] // 32
    along_x = jnp.where(rows == lanes, jnp.tile(half_x, (3, 4)), 0.0)
    blocks = jnp.arange(256, dtype=jnp.int32) // 64
    stacked = jnp.tile(jnp.concatenate([own[2], own[1], own[1], own[2]], axis=0), (1, 4))
    block_basis = jnp.where(blocks[:, None] == blocks[None, :], stacked, 0.0)

    def spread(column):
        return jnp.broadcast_to(column[:, None], (64, LANES))

    lane = jnp.arange(LANES, dtype=jnp.int32)
    pad = lane >= 96
    weights = jnp.where(
        pad[:, None], 0.0, jnp.concatenate([jnp.repeat(own_coeffs, 32, axis=0), own_coeffs[:1].repeat(32, axis=0)], axis=0)
    )
    half_values = lax.dynamic_slice(own_values[0], (half * 32,), (32,))
    x_term = jnp.where(pad, 1.0, weights[:, 0] * jnp.tile(half_values, 4))
    xy_term = x_term[None, :] + weights[None, :, 1] * own_values[1][:, None]
    z_term = weights[None, :, 2] * own_values[2][:, None]
    constants = jnp.stack(
        [
            spread(own[1][0]),
            spread(own[1][63]),
            spread(own[2][0]),
            spread(own[2][63]),
            xy_term,
            z_term,
        ]
    )
    return along_x.T, along_x, block_basis.T, block_basis, constants


def body(
    mult_iterate,
    residual,
    direction,
    mult_scale,
    eigen_basis,
    eigen_values,
    elastic_coef,
    coarse_inverse,
    send_pos,
    pair_slots,
    prim_rows,
    coarse_idx,
):
    group = lax.axis_index("group")
    pencil = lax.axis_index("pencil")
    groups = lax.axis_size("group")
    pencils = lax.axis_size("pencil")
    iterate_now = mult_iterate.reshape(64, LANES)
    resid_now = residual.reshape(64, LANES)
    search_dir = direction.reshape(64, LANES)
    scale_now = mult_scale.reshape(64, LANES)
    pair_rows = pair_slots.reshape(128, LANES)
    slots = slot_index(send_pos.reshape(128, LANES))
    primal = prim_rows[0, 0]
    coarse_ids = coarse_idx[0, 0]

    lane_group = jnp.arange(LANES, dtype=jnp.int32) // 32
    mine = lane_group == group % 4
    extra = jnp.zeros((8, LANES), F32)
    extra = extra.at[0].set(jnp.where(mine, jnp.tile(primal, 4), 0).astype(F32))
    extra = extra.at[1].set(jnp.where(mine, jnp.tile(coarse_ids, 4), 0).astype(F32))

    index_scratch = [pltpu.VMEM((128, LANES), F32), pltpu.VMEM((128, LANES), F32)]
    back = call(
        back_kernel,
        jax.ShapeDtypeStruct((groups, 8, LANES), F32),
        3,
        "back",
        index_scratch + [pltpu.VMEM((2, 128, LANES), F32), pltpu.VMEM((128, LANES), F32)],
    )(pair_rows, search_dir, extra)
    arrived = exchange(back, "group")

    loads = call(
        load_kernel,
        jax.ShapeDtypeStruct((pencils, 24, 256), F32),
        2,
        "load",
        index_scratch + [pltpu.VMEM((2, 256, LANES), F32), pltpu.VMEM((192, LANES), F32)],
    )(arrived, slots)
    columns = exchange(loads, "pencil")

    constants = solve_constants(eigen_basis, eigen_values, elastic_coef, pencil)
    partial = call(
        solve_kernel,
        jax.ShapeDtypeStruct((pencils, 24, 256), F32),
        6,
        "solve",
        [
            pltpu.VMEM((256, LANES), F32),
            pltpu.VMEM((64, 8, LANES), F32),
            pltpu.VMEM((64, 8, LANES), F32),
        ],
    )(columns, *constants)
    slabs = exchange(partial, "pencil")

    primal_slots = slots.reshape(-1)[primal]
    extra_slots = jnp.full((16, LANES), -1, jnp.int32)
    extra_slots = extra_slots.at[0].set(jnp.where(mine, jnp.tile(primal_slots, 4), -1))
    picked = call(
        pick_kernel,
        jax.ShapeDtypeStruct((groups, 8, LANES), F32),
        2,
        "pick",
        [pltpu.VMEM((192, LANES), F32), pltpu.VMEM((144, LANES), F32)],
    )(slabs, jnp.concatenate([slots, extra_slots], axis=0))
    owner = exchange(picked, "group")

    packed = jnp.sum(arrived[:, 4:6, :].reshape(8, 4, 2, LANES), axis=1).astype(jnp.int32)
    their_primal = packed[:, 0]
    their_ids = packed[:, 1]
    sender = 4 * jnp.arange(8, dtype=jnp.int32)[:, None] + lane_group[None, :]
    local = their_primal - group * 512
    valid = (local >= 0) & (local < 512)
    place = jnp.where(valid, (sender * 8 + local // LANES) * LANES + local % LANES, -1)

    small_index = [pltpu.VMEM((8, LANES), F32), pltpu.VMEM((8, LANES), F32)]
    coarse_part = call(
        coarse_kernel,
        jax.ShapeDtypeStruct((pencils, 8, LANES), F32),
        2,
        "coarse",
        small_index + [pltpu.VMEM((3, 8, LANES), F32)],
    )(owner, their_ids)
    coarse_all = exchange(coarse_part, "pencil")

    image, sums = call(
        image_kernel,
        (
            jax.ShapeDtypeStruct((64, LANES), F32),
            jax.ShapeDtypeStruct((groups * pencils, LANES), F32),
        ),
        9,
        "image",
        [pltpu.VMEM((8, LANES), F32), pltpu.VMEM((LANES, LANES), F32)]
        + small_index
        + [pltpu.VMEM((3, 8, LANES), F32), pltpu.VMEM((256, LANES), F32)],
    )(
        coarse_all, coarse_inverse, their_ids, place, owner, pair_rows, search_dir, resid_now,
        scale_now,
    )
    totals = exchange(sums, ("group", "pencil"))

    shape = jax.ShapeDtypeStruct((64, LANES), F32)
    outs = call(update_kernel, (shape, shape, shape), 6, "update")(
        totals, iterate_now, resid_now, search_dir, scale_now, image
    )
    return tuple(out.reshape(1, 1, -1) for out in outs)


def solution(mesh):
    in_specs = (
        P("group", "pencil", None),
        P("group", "pencil", None),
        P("group", "pencil", None),
        P("group", "pencil", None),
        P("group", None, None, None),
        P("group", None, None),
        P("group", None, None),
        P(),
        P("group", "pencil", None),
        P("group", "pencil", None, None),
        P("group", "pencil", None),
        P("group", "pencil", None),
    )
    out_specs = (P("group", "pencil", None), P("group", "pencil", None), P("group", "pencil", None))
    return jax.shard_map(body, mesh=mesh, in_specs=in_specs, out_specs=out_specs, check_vma=False)
```

time: 881 us -> 138 us (0.16)
  local copies, waits for them, and re-layouts: 521 us -> 14.4 us
  blocking collectives: 220 us -> 20.1 us
  matrix products: 33.9 us -> 0 us
  Pallas kernels: 0 us -> 33.7 us
  waiting for transfers between devices: 54.7 us -> 23.4 us
    gather x4 -> x1, local copies, waits for them, and re-layouts: 253 us -> 0.7 us  [body(): primal_slots = slots.reshape(-1)[primal]]
    psum x3 -> x0, blocking collectives: 220 us -> none  [the longest x1 74 us: body(): norm_next = lax.psum(jnp.sum(resid_next * precond), ('group', 'pencil'))]
    scatter x3 -> x2, local copies, waits for them, and re-layouts: 124 us -> 0.04 us  [the longest x1 0.04 us: body(): extra.at[1].set(jnp.where(mine, jnp.tile(coarse_ids, 4), 0).astype(F32))]
    unnamed x40 -> x25, local copies, waits for them, and re-layouts: 70.6 us -> 4.36 us
    reshape x5 -> x3, local copies, waits for them, and re-layouts: 44 us -> 1.68 us  [the longest x1 1.53 us: body(): pair_rows = pair_slots.reshape(128, LANES)]
    dot_general x9 -> x0, matrix products: 33.9 us -> none  [the longest x1 5.64 us: body(): lifted = jnp.dot(coarse_inverse, total_coarse, precision=highest)]
    pallas_call x0 -> x7, Pallas kernels: none -> 33.7 us  [the longest x1 7.45 us: body(): call(image_kernel, (jax.ShapeDtypeStruct((64, LANES), F32), jax.ShapeDtyp...]
    all_to_all x4 -> x5, waiting for transfers between devices: 54.7 us -> 23.4 us  [exchange(): return lax.all_to_all(array, axis, split_axis=0, concat_axis=0, tiled=True)]
  transfers between devices with their start and end apart: 4 -> 5, of which waited for: 4 -> 4; matrix products, arithmetic and copies ran while one was open for 0% -> 11% of each run, Pallas kernels for 0% -> 0%
where the time goes in v1:
time: 138 us; the launch traced here: 137 us
  starting transfers between devices  36.6 us (27%)
  Pallas kernels  33.7 us (24%)
  waiting for transfers between devices  23.4 us (17%)
  blocking collectives  20.1 us (15%)
  local copies, waits for them, and re-layouts  14.4 us (10%)
  other arithmetic  7.71 us (6%)
    all_to_all x5, starting transfers between devices, exchange(): return lax.all_to_all(array, axis, split_axis=0, concat_axis=0, tiled=True)  36.6 us
    all_to_all x5, waiting for transfers between devices, exchange(): return lax.all_to_all(array, axis, split_axis=0, concat_axis=0, tiled=True)  23.4 us
    all_to_all x1, blocking collectives, exchange(): return lax.all_to_all(array, axis, split_axis=0, concat_axis=0, tiled=True)  20.1 us
    pallas_call x1, Pallas kernels, body(): call(image_kernel, (jax.ShapeDtypeStruct((64, LANES), F32), jax.ShapeDtyp...  7.45 us
    pallas_call x1, Pallas kernels, body(): call(pick_kernel, jax.ShapeDtypeStruct((groups, 8, LANES), F32), 2, 'pick...  6.27 us
    pallas_call x1, Pallas kernels, body(): call(load_kernel, jax.ShapeDtypeStruct((pencils, 24, 256), F32), 2, 'load...  5.71 us
    pallas_call x1, Pallas kernels, body(): call(solve_kernel, jax.ShapeDtypeStruct((pencils, 24, 256), F32), 6, 'sol...  5.36 us
    pallas_call x1, Pallas kernels, body(): call(back_kernel, jax.ShapeDtypeStruct((groups, 8, LANES), F32), 3, 'back...  5.34 us
  transfers between devices with their start and end apart: 5, of which 4 were waited for; matrix products, arithmetic and copies ran while one was open for 11% of the time, Pallas kernels for 0%

profile of v1, /device:TPU:1, one launch (start us, length us, event | category | flops | bytes accessed | tf_op | source)
XLA Modules:
  0.0 136.9 jit_solution(7221070740342964090)
XLA Ops:
  0.7 0.7 tile.64
  1.4 0.7 tile.61
  2.1 1.5 %reshape.529.idx_ref.pair_ref = s32[128,128]{1,0:T(8,128)} reshape(s32[1,1,2,8192]{3,2,1,0:T(2,128)} %param.27) | data formatting | bytes 131072 | tf_op jit(solution)/shard_map/reshape | solution.py:424
  3.7 0.6 copy-done.8
  4.3 5.3 %back.1 = f32[32,8,128]{2,1,0:T(8,128)} custom-call(s32[128,128]{1,0:T(8,128)} %reshape.529.idx_ref.pair_ref, f32[64,128]{1,0:T(8,128)} %bitcast.78, f32[8,128]{1,0:T(8,128)} %copy-done.8), custom_call_target="tpu_custom_call" | custom-call | flops 1000000 | bytes 262144 | tf_op jit(solution)/shard_map/back/pallas_call | solution.py:436
  9.7 12.0 %all-to-all-start = ((f32[32,8,128]{2,1,0:T(8,128)}), f32[32,8,128]{2,1,0:T(8,128)S(1)}, u32[]{:S(2)}, u32[]{:S(2)}) async-start(f32[32,8,128]{2,1,0:T(8,128)} %back.1), calls=%async_computation | async-start | bytes 262144 | tf_op jit(solution)/shard_map/all_to_all | solution.py:361
  21.7 0.7 fusion.38
  22.5 1.1 compare_reduce_fusion
  23.6 1.1 broadcast_divide_fusion
  24.7 0.8 constant_dynamic-slice_fusion.11
  25.6 0.2 tile.68
  25.9 0.1 fusion.49
  26.0 0.7 compare_select_fusion.1.bx_ref
  26.9 0.8 constant_dynamic-slice_fusion.5
  27.6 0.7 fusion.39
  28.4 0.7 fusion.40
  29.7 0.3 fusion.13
  30.0 0.7 gather_fusion
  30.9 0.1 copy.38
  31.2 0.3 fusion.5.idx_ref
  31.6 0.1 fusion.48
  31.8 0.6 select_add_fusion.idx_ref
  32.5 0.8 copy.40.bxt_ref
  33.2 0.8 copy.41.bdt_ref
  34.0 0.8 compare_select_fusion.bd_ref
  34.8 0.6 copy-done.4
  35.5 5.7 %load.1 = f32[8,24,256]{2,1,0:T(8,128)} custom-call(f32[32,8,128]{2,1,0:T(8,128)} %copy-done.4, s32[128,128]{1,0:T(8,128)} %copy-done.5), custom_call_target="tpu_custom_call" | custom-call | flops 1000000 | bytes 262144 | tf_op jit(solution)/shard_map/load/pallas_call | solution.py:445
  41.2 5.2 %all-to-all-start.1 = ((f32[8,24,256]{2,1,0:T(8,128)}), f32[8,24,256]{2,1,0:T(8,128)S(1)}, u32[]{:S(2)}, u32[]{:S(2)}) async-start(f32[8,24,256]{2,1,0:T(8,128)} %load.1), calls=%async_computation.1 | async-start | bytes 393216 | tf_op jit(solution)/shard_map/all_to_all | solution.py:361
  46.5 5.8 %all-to-all-done.1.recv_ref = f32[8,24,256]{2,1,0:T(8,128)S(1)} async-done(((f32[8,24,256]{2,1,0:T(8,128)}), f32[8,24,256]{2,1,0:T(8,128)S(1)}, u32[]{:S(2)}, u32[]{:S(2)}) %all-to-all-start.1) | async-done | bytes 196640 | tf_op jit(solution)/shard_map/all_to_all | solution.py:361
  52.3 0.7 copy-done.3
  53.0 5.4 %solve.1 = f32[8,24,256]{2,1,0:T(8,128)} custom-call(f32[8,24,256]{2,1,0:T(8,128)} %copy-done.3, f32[128,192]{1,0:T(8,128)} %copy.40.bxt_ref, f32[192,128]{1,0:T(8,128)} %compare_select_fusion.1.bx_ref, f32[256,256]{1,0:T(8,128)} %copy.41.bdt_ref, f32[256,256]{1,0:T(8,128)} %compare_select_fusion.bd_ref, f32[6,64,128]{2,1,0:T(8,128)} %copy-done.6), custom_call_target="tpu_custom_call" | custom-call | flops 1000000 | bytes 262144 | tf_op jit(solution)/shard_map/solve/pallas_call | solution.py:455
  58.3 4.2 %all-to-all-start.2 = ((f32[8,24,256]{2,1,0:T(8,128)}), f32[8,24,256]{2,1,0:T(8,128)S(1)}, u32[]{:S(2)}, u32[]{:S(2)}) async-start(f32[8,24,256]{2,1,0:T(8,128)} %solve.1), calls=%async_computation.2 | async-start | bytes 393216 | tf_op jit(solution)/shard_map/all_to_all | solution.py:361
  62.6 0.9 bitcast_reduce_fusion
  63.5 4.9 %all-to-all-done.2.recv_ref = f32[8,24,256]{2,1,0:T(8,128)S(1)} async-done(((f32[8,24,256]{2,1,0:T(8,128)}), f32[8,24,256]{2,1,0:T(8,128)S(1)}, u32[]{:S(2)}, u32[]{:S(2)}) %all-to-all-start.2) | async-done | bytes 196640 | tf_op jit(solution)/shard_map/all_to_all | solution.py:361
  68.5 0.7 copy-done.2
  69.1 6.3 %pick.1 = f32[32,8,128]{2,1,0:T(8,128)} custom-call(f32[8,24,256]{2,1,0:T(8,128)} %copy-done.2, s32[144,128]{1,0:T(8,128)} %select_add_fusion.idx_ref), custom_call_target="tpu_custom_call" | custom-call | flops 1000000 | bytes 262144 | tf_op jit(solution)/shard_map/pick/pallas_call | solution.py:471
  75.4 9.5 %all-to-all-start.3 = ((f32[32,8,128]{2,1,0:T(8,128)}), f32[32,8,128]{2,1,0:T(8,128)S(1)}, u32[]{:S(2)}, u32[]{:S(2)}) async-start(f32[32,8,128]{2,1,0:T(8,128)} %pick.1), calls=%async_computation.3 | async-start | bytes 262144 | tf_op jit(solution)/shard_map/all_to_all | solution.py:361
  84.9 0.6 slice_bitcast_fusion.ids_ref
  85.5 8.6 %all-to-all-done.3.arr_ref = f32[32,8,128]{2,1,0:T(8,128)S(1)} async-done(((f32[32,8,128]{2,1,0:T(8,128)}), f32[32,8,128]{2,1,0:T(8,128)S(1)}, u32[]{:S(2)}, u32[]{:S(2)}) %all-to-all-start.3) | async-done | bytes 131104 | tf_op jit(solution)/shard_map/all_to_all | solution.py:361
  94.1 0.6 copy-done.1
  94.7 1.9 %coarse.1 = f32[8,8,128]{2,1,0:T(8,128)} custom-call(f32[32,8,128]{2,1,0:T(8,128)} %copy-done.1, s32[8,128]{1,0:T(8,128)} %slice_bitcast_fusion.ids_ref), custom_call_target="tpu_custom_call" | custom-call | flops 1000000 | bytes 262144 | tf_op jit(solution)/shard_map/coarse/pallas_call | solution.py:489
  96.6 5.6 %all-to-all-start.4 = ((f32[8,8,128]{2,1,0:T(8,128)}), f32[8,8,128]{2,1,0:T(8,128)S(1)}, u32[]{:S(2)}, u32[]{:S(2)}) async-start(f32[8,8,128]{2,1,0:T(8,128)} %coarse.1), calls=%async_computation.4 | async-start | bytes 65536 | tf_op jit(solution)/shard_map/all_to_all | solution.py:361
  102.2 0.7 fusion.31.place_ref
  102.9 4.1 %all-to-all-done.4.coarse_ref = f32[8,8,128]{2,1,0:T(8,128)S(1)} async-done(((f32[8,8,128]{2,1,0:T(8,128)}), f32[8,8,128]{2,1,0:T(8,128)S(1)}, u32[]{:S(2)}, u32[]{:S(2)}) %all-to-all-start.4) | async-done | bytes 32800 | tf_op jit(solution)/shard_map/all_to_all | solution.py:361
  106.9 0.6 copy-done.7
  107.5 7.5 %image.1 = (f32[64,128]{1,0:T(8,128)}, f32[256,128]{1,0:T(8,128)}) custom-call(f32[8,8,128]{2,1,0:T(8,128)} %copy-done.7, f32[1024,1024]{1,0:T(8,128)} %inv_ref.1, s32[8,128]{1,0:T(8,128)} %slice_bitcast_fusion.ids_ref, s32[8,128]{1,0:T(8,128)} %fusion.31.place_ref, f32[32,8,128]{2,1,0:T(8,128)} %copy-done.1, s32[128,128]{1,0:T(8,128)} %reshape.529.idx_ref.pair_ref, ...), custom_call_target="tpu_custom_call" | custom-call | flops 1000000 | bytes 262144 | tf_op jit(solution)/shard_map/image/pallas_call | solution.py:498
  115.0 20.1 %all_to_all.36 = f32[256,1,128]{2,1,0:T(1,128)} all-to-all(f32[256,1,128]{2,1,0:T(1,128)} %bitcast.85), channel_id=1, replica_groups=mesh['group'=32,'pencil'=8] {'group','pencil'}, dimensions={0} | all-to-all | bytes 262144 | tf_op jit(solution)/shard_map/all_to_all | solution.py:361
  135.1 1.7 %update.1 = (f32[64,128]{1,0:T(8,128)}, f32[64,128]{1,0:T(8,128)}, f32[64,128]{1,0:T(8,128)}) custom-call(f32[256,128]{1,0:T(8,128)} %bitcast.77, f32[64,128]{1,0:T(8,128)} %bitcast.89, f32[64,128]{1,0:T(8,128)} %bitcast.82, f32[64,128]{1,0:T(8,128)} %bitcast.80, f32[64,128]{1,0:T(8,128)} %bitcast.84, f32[64,128]{1,0:T(8,128)} %get-tuple-element.45.image_ref), custom_call_target="tpu_custom_call" | custom-call | flops 1000000 | bytes 262144 | tf_op jit(solution)/shard_map/update/pallas_call | solution.py:516
  (53 shorter events, 1.9 us)
Async XLA Ops:
  0.6 21.8 %copy-start = (f32[4,3,3]{2,0,1:T(4,128)S(1)}, f32[4,3,3]{2,0,1:T(4,128)}, u32[]{:S(2)}) copy-start(f32[4,3,3]{2,0,1:T(4,128)} %param.24) | copy-start | bytes 436
  3.7 0.6 copy-start.8
  9.7 25.2 %all-to-all-start = ((f32[32,8,128]{2,1,0:T(8,128)}), f32[32,8,128]{2,1,0:T(8,128)S(1)}, u32[]{:S(2)}, u32[]{:S(2)}) async-start(f32[32,8,128]{2,1,0:T(8,128)} %back.1), calls=%async_computation | async-start | bytes 262144 | tf_op jit(solution)/shard_map/all_to_all | solution.py:361
  31.4 3.4 %copy-start.5 = (s32[128,128]{1,0:T(8,128)}, s32[128,128]{1,0:T(8,128)S(1)}, u32[]{:S(2)}) copy-start(s32[128,128]{1,0:T(8,128)S(1)} %fusion.5.idx_ref) | copy-start | bytes 196612
  34.8 0.6 copy-start.4
  41.2 11.1 %all-to-all-start.1 = ((f32[8,24,256]{2,1,0:T(8,128)}), f32[8,24,256]{2,1,0:T(8,128)S(1)}, u32[]{:S(2)}, u32[]{:S(2)}) async-start(f32[8,24,256]{2,1,0:T(8,128)} %load.1), calls=%async_computation.1 | async-start | bytes 393216 | tf_op jit(solution)/shard_map/all_to_all | solution.py:361
  46.5 5.8 %copy-start.6 = (f32[6,64,128]{2,1,0:T(8,128)}, f32[6,64,128]{2,1,0:T(8,128)S(1)}, u32[]{:S(2)}) copy-start(f32[6,64,128]{2,1,0:T(8,128)S(1)} %multiply_dynamic-update-slice_fusion.cst_ref) | copy-start | bytes 589828
  52.3 0.7 copy-start.3
  58.3 10.1 %all-to-all-start.2 = ((f32[8,24,256]{2,1,0:T(8,128)}), f32[8,24,256]{2,1,0:T(8,128)S(1)}, u32[]{:S(2)}, u32[]{:S(2)}) async-start(f32[8,24,256]{2,1,0:T(8,128)} %solve.1), calls=%async_computation.2 | async-start | bytes 393216 | tf_op jit(solution)/shard_map/all_to_all | solution.py:361
  68.5 0.7 copy-start.2
  75.4 18.7 %all-to-all-start.3 = ((f32[32,8,128]{2,1,0:T(8,128)}), f32[32,8,128]{2,1,0:T(8,128)S(1)}, u32[]{:S(2)}, u32[]{:S(2)}) async-start(f32[32,8,128]{2,1,0:T(8,128)} %pick.1), calls=%async_computation.3 | async-start | bytes 262144 | tf_op jit(solution)/shard_map/all_to_all | solution.py:361
  94.1 0.7 copy-start.1
  96.6 10.3 %all-to-all-start.4 = ((f32[8,8,128]{2,1,0:T(8,128)}), f32[8,8,128]{2,1,0:T(8,128)S(1)}, u32[]{:S(2)}, u32[]{:S(2)}) async-start(f32[8,8,128]{2,1,0:T(8,128)} %coarse.1), calls=%async_computation.4 | async-start | bytes 65536 | tf_op jit(solution)/shard_map/all_to_all | solution.py:361
  106.9 0.6 copy-start.7

commit v2 on v0

v2 whole, which is shorter than its diff:
```python
import jax
import jax.numpy as jnp
from jax import lax
from jax.experimental import pallas as pl
from jax.experimental.pallas import tpu as pltpu
from jax.sharding import PartitionSpec as P

LANES = 128
BF16 = jnp.bfloat16
F32 = jnp.float32
HIGHEST = lax.Precision.HIGHEST
VMEM = pl.BlockSpec(memory_space=pltpu.VMEM)


HBM = pl.BlockSpec(memory_space=pltpu.HBM)


def call(kernel, out_shape, in_specs, name, scratch=(), flops=4_000_000):
    single = not isinstance(out_shape, (tuple, list))
    return pl.pallas_call(
        kernel,
        out_shape=out_shape,
        in_specs=in_specs,
        out_specs=VMEM if single else [VMEM] * len(out_shape),
        scratch_shapes=list(scratch),
        name=name,
        compiler_params=pltpu.CompilerParams(vmem_limit_bytes=16 << 20),
        cost_estimate=pl.CostEstimate(flops=flops, bytes_accessed=1 << 18, transcendentals=0),
    )


def split_channels(value, count):
    pieces = []
    for _ in range(count):
        piece = value.astype(BF16).astype(F32)
        pieces.append(piece)
        value = value - piece
    return pieces


def one_hot_parts(rows, high_row, low_row, piece_rows, chunk, channels):
    row_ids = lax.broadcasted_iota(jnp.int32, (rows, LANES), 0).astype(F32).astype(BF16)
    lane_ids = lax.broadcasted_iota(jnp.int32, (LANES, LANES), 0).astype(F32).astype(BF16)
    left, right = [], []
    for r in range(chunk):
        high = jnp.broadcast_to(high_row(r), (rows, LANES)).astype(BF16)
        low = jnp.broadcast_to(low_row(r), (LANES, LANES)).astype(BF16)
        left.append(jnp.where(row_ids == high, BF16(1), BF16(0)))
        match = lane_ids == low
        pieces = [
            jnp.where(
                match, jnp.broadcast_to(piece_rows(n, r), (LANES, LANES)).astype(BF16), BF16(0)
            )
            for n in range(channels)
        ]
        right.append(jnp.concatenate(pieces, axis=0))
    return jnp.concatenate(left, axis=1), jnp.concatenate(right, axis=1)


def pair_dot(left, right):
    return lax.dot_general(left, right, (((1,), (1,)), ((), ())), preferred_element_type=F32)


def scatter_large(rows, high_ref, low_ref, piece_row, total, chunk):
    def step(index, acc):
        left, right = one_hot_parts(
            rows,
            lambda r: high_ref[pl.ds(index * chunk + r, 1), :],
            lambda r: low_ref[pl.ds(index * chunk + r, 1), :],
            lambda n, r: piece_row(n, index, r),
            chunk,
            2,
        )
        return acc + pair_dot(right, left)

    acc = lax.fori_loop(0, total // chunk, step, jnp.zeros((2 * LANES, rows), F32))
    return (acc[:LANES] + acc[LANES:]).T


def scatter_small(rows, high_ref, low_ref, piece_ref, count):
    left, right = one_hot_parts(
        rows,
        lambda r: high_ref[r : r + 1, :],
        lambda r: low_ref[r : r + 1, :],
        lambda n, r: piece_ref[n, r : r + 1, :],
        count,
        3,
    )
    acc = pair_dot(left, right)
    return acc[:, :LANES] + acc[:, LANES : 2 * LANES] + acc[:, 2 * LANES :]


def gather_rows(indices, table_row, table_rows):
    high = lax.shift_right_arithmetic(indices, 7)
    low = jnp.bitwise_and(indices, LANES - 1)
    acc = [jnp.zeros(indices.shape, F32) for _ in range(2)]
    for a in range(table_rows):
        row = jnp.broadcast_to(table_row(a), indices.shape)
        picked = jnp.take_along_axis(row, low, axis=1, mode="promise_in_bounds")
        acc[a % 2] = jnp.where(high == a, picked, acc[a % 2])
    return acc[0] + acc[1]


def store_digits(idx, high_ref, low_ref):
    high_ref[...] = lax.shift_right_arithmetic(idx, 7).astype(F32)
    low_ref[...] = jnp.bitwise_and(idx, LANES - 1).astype(F32)


def floor_div(value, divisor):
    return jnp.floor((value + 0.5) * (1.0 / divisor))


def cell_digits(cells):
    cells = cells.astype(F32)
    plane = floor_div(cells, 252)
    spot = cells - 252.0 * plane
    slot = (
        spot
        + jnp.where(spot >= 64.0, 1.0, 0.0)
        + jnp.where(spot >= 126.0, 2.0, 0.0)
        + jnp.where(spot >= 188.0, 1.0, 0.0)
    )
    along_x = floor_div(plane, 12)
    rest = plane - 12.0 * along_x
    patch = floor_div(rest, 3)
    component = rest - 3.0 * patch
    half = jnp.where(slot >= 128.0, 1.0, 0.0)
    return patch, component, along_x, half, slot - 128.0 * half


def own_lanes():
    lane = lax.broadcasted_iota(jnp.int32, (1, LANES), 1)
    return lax.shift_right_logical(lane, 5)


def spread_lanes(row):
    return jnp.concatenate([row] * 4, axis=1)


CHUNK = 32
OWNER_ROWS = 14


def start_copies(pairs, sems):
    copies = [
        pltpu.make_async_copy(source, target, sems.at[n])
        for n, (source, target) in enumerate(pairs)
    ]
    for copy in copies:
        copy.start()
    return copies


def back_kernel(
    pair_hbm, dir_hbm, cells_hbm, prim_hbm, ids_hbm, basis_hbm, values_hbm, coeff_hbm,
    out_ref, idx_ref, cells_ref, small_ref, bxt_ref, bx_ref, bdt_ref, bd_ref, cst_ref,
    pair_ref, dir_ref, prim_ref, ids_ref, basis_ref, values_ref, coeff_ref,
    high_ref, low_ref, piece_ref, sems,
):
    pencil = lax.axis_index("pencil")
    patch = lax.div(pencil, 2)
    side = lax.rem(pencil, 2)
    copies = start_copies(
        [
            (pair_hbm, pair_ref),
            (dir_hbm, dir_ref),
            (cells_hbm, cells_ref),
            (prim_hbm, prim_ref),
            (ids_hbm, ids_ref),
            (basis_hbm.at[patch], basis_ref),
            (values_hbm, values_ref),
            (coeff_hbm, coeff_ref),
        ],
        sems,
    )
    half = dir_ref.shape[0]
    bx_ref[...] = jnp.zeros(bx_ref.shape, F32)
    bxt_ref[...] = jnp.zeros(bxt_ref.shape, F32)
    bd_ref[...] = jnp.zeros(bd_ref.shape, F32)
    bdt_ref[...] = jnp.zeros(bdt_ref.shape, F32)
    copies[0].wait()
    copies[1].wait()
    for k in range(half):
        both = pair_ref[:, k * LANES : (k + 1) * LANES]
        idx_ref[k : k + 1, :] = both[0:1]
        idx_ref[half + k : half + k + 1, :] = both[1:2]
    store_digits(idx_ref[...], high_ref, low_ref)
    for n, piece in enumerate(split_channels(dir_ref[...], 2)):
        piece_ref[n, :half, :] = piece
        piece_ref[n, half:, :] = -piece
    out_ref[...] = scatter_large(
        2 * half,
        high_ref,
        low_ref,
        lambda n, t, r: piece_ref[n, pl.ds(t * CHUNK + r, 1), :],
        2 * half,
        CHUNK,
    )
    for copy in copies[2:]:
        copy.wait()
    small_ref[...] = jnp.zeros(small_ref.shape, F32)
    small_ref[0:1, :] = spread_lanes(prim_ref[...].astype(F32))
    small_ref[1:2, :] = spread_lanes(ids_ref[...].astype(F32))
    along_x, along_y, along_z = basis_ref[0], basis_ref[1], basis_ref[2]
    first = lax.broadcasted_iota(jnp.int32, (64, 64), 0)
    second = lax.broadcasted_iota(jnp.int32, (64, 64), 1)
    identity = jnp.where(first == second, 1.0, 0.0)
    half_x = jnp.where(side == 1, along_x[:, 32:64], along_x[:, 0:32])
    flipped = full_dot(identity, along_x, ((1,), (1,)))
    half_flipped = jnp.where(side == 1, flipped[32:64], flipped[0:32])
    for c in range(3):
        bx_ref[64 * c : 64 * c + 64, 32 * c : 32 * c + 32] = half_x
        bxt_ref[32 * c : 32 * c + 32, 64 * c : 64 * c + 64] = half_flipped
    flipped_y = full_dot(identity, along_y, ((1,), (1,)))
    flipped_z = full_dot(identity, along_z, ((1,), (1,)))
    for block in range(4):
        part = slice(64 * block, 64 * block + 64)
        bd_ref[part, part] = along_z if block in (0, 3) else along_y
        bdt_ref[part, part] = flipped_z if block in (0, 3) else flipped_y

    def spread(column):
        return jnp.broadcast_to(column, (64, LANES))

    cst_ref[0] = spread(column_of(along_y[0:1]))
    cst_ref[1] = spread(column_of(along_y[63:64]))
    cst_ref[2] = spread(column_of(along_z[0:1]))
    cst_ref[3] = spread(column_of(along_z[63:64]))
    lane = lax.broadcasted_iota(jnp.int32, (1, LANES), 1)

    def weight(dim):
        value = jnp.zeros((1, LANES), F32)
        for c in range(3):
            here = lax.shift_right_logical(lane, 5) == c
            coeff = coeff_ref[c, pl.ds(patch, 1), :][:, dim : dim + 1]
            value = jnp.where(here, jnp.broadcast_to(coeff, (1, LANES)), value)
        return value

    x_values, y_values, z_values = (values_ref[dim, pl.ds(patch, 1), :] for dim in range(3))
    half_values = jnp.where(side == 1, x_values[:, 32:64], x_values[:, 0:32])
    x_term = jnp.where(lane >= 96, 1.0, weight(0) * spread_lanes(half_values))
    y_term = weight(1) * spread(column_of(y_values))
    cst_ref[4] = x_term + y_term
    cst_ref[5] = weight(2) * spread(column_of(z_values))


def load_kernel(
    arr_ref, pos_ref, small_ref, out_ref, slots_ref, high_ref, low_ref, piece_ref, acc_ref
):
    patch, component, along_x, half, lane = cell_digits(pos_ref[...])
    row = patch * 48.0 + half * 24.0 + component * 8.0 + along_x
    high_ref[...] = row
    low_ref[...] = lane
    slots_ref[...] = (row * 128.0 + lane).astype(jnp.int32)
    rows = pos_ref.shape[0]
    for n, piece in enumerate(split_channels(arr_ref[...], 2)):
        piece_ref[n] = piece
    acc_ref[...] = scatter_large(
        acc_ref.shape[0],
        high_ref,
        low_ref,
        lambda n, t, r: piece_ref[n, pl.ds(t * CHUNK + r, 1), :],
        rows,
        CHUNK,
    )
    pencil = lax.axis_index("pencil")
    mine = own_lanes() == lax.rem(pencil, 4)
    primal = jnp.broadcast_to(small_ref[0:1, :], (8, LANES)).astype(jnp.int32)
    cells = gather_rows(primal, lambda a: pos_ref[a : a + 1, :].astype(F32), rows)
    patch, component, along_x, half, lane = cell_digits(cells[0:1])
    place = half * 192.0 + component * 64.0 + along_x + (8 * pencil).astype(F32)
    code = place * 128.0 + lane
    ids = jnp.where(mine, small_ref[1:2, :], 0.0)
    for dest in range(out_ref.shape[0]):
        for side in range(2):
            start = (dest // 2) * 48 + side * 24
            out_ref[dest, 0:24, side * LANES : (side + 1) * LANES] = acc_ref[start : start + 24, :]
        own = jnp.where(patch == float(dest // 2), code, -1.0)
        out_ref[dest, 24:32, :] = jnp.zeros((8, 256), F32)
        out_ref[dest, 24:25, 0:LANES] = jnp.where(mine, own, 0.0)
        out_ref[dest, 24:25, LANES:] = ids


def full_dot(left, right, contract):
    return lax.dot_general(
        left, right, ((contract[0], contract[1]), ((), ())), precision=HIGHEST,
        preferred_element_type=F32,
    )


def column_of(row):
    count = row.shape[1]
    first = lax.broadcasted_iota(jnp.int32, (count, count), 0)
    second = lax.broadcasted_iota(jnp.int32, (count, count), 1)
    spread = jnp.broadcast_to(row, (count, count))
    return jnp.sum(jnp.where(first == second, spread, 0.0), axis=1, keepdims=True)


def solve_kernel(
    recv_ref, bxt_ref, bx_ref, bdt_ref, bd_ref, cst_ref, out_ref, fwd_ref, d0_ref, d1_ref,
    slab_ref, high_ref, low_ref, piece_ref,
):
    sources = recv_ref.shape[0]
    load = jnp.concatenate(
        [recv_ref[src, 8 * c : 8 * c + 8, :] for c in range(3) for src in range(sources)], axis=0
    )
    along_x = full_dot(bxt_ref[...], load, ((1,), (0,)))
    fwd_ref[...] = full_dot(bdt_ref[...], along_x, ((1,), (1,)))

    def step(j, carry):
        top, bottom = carry

        def row(index):
            return jnp.broadcast_to(cst_ref[index, pl.ds(j, 1), :], (64, LANES))

        first = jnp.broadcast_to(fwd_ref[pl.ds(64 + j, 1), :], (64, LANES))
        last = jnp.broadcast_to(fwd_ref[pl.ds(128 + j, 1), :], (64, LANES))
        y_first, y_last = row(0), row(1)
        spectral = (
            y_first * fwd_ref[0:64, :]
            + y_last * fwd_ref[192:256, :]
            + first * cst_ref[2]
            + last * cst_ref[3]
        )
        scaled = spectral / (row(4) + cst_ref[5])
        along_first = cst_ref[2] * scaled
        along_last = cst_ref[3] * scaled
        d0_ref[j] = jnp.sum(along_first.reshape(8, 8, LANES), axis=0)
        d1_ref[j] = jnp.sum(along_last.reshape(8, 8, LANES), axis=0)
        return top + y_first * scaled, bottom + y_last * scaled

    zero = jnp.zeros((64, LANES), F32)
    top, bottom = lax.fori_loop(0, 64, step, (zero, zero), unroll=4)
    edges = jnp.concatenate(
        [top, jnp.sum(d0_ref[...], axis=1), jnp.sum(d1_ref[...], axis=1), bottom], axis=0
    )
    cells = full_dot(bd_ref[...], edges, ((1,), (0,)))
    slab_ref[...] = full_dot(bx_ref[...], cells, ((1,), (1,)))

    def packed(lanes):
        halves = []
        for part in range(2):
            row = recv_ref[4 * part, 24:25, lanes]
            for k in range(1, 4):
                row = row + recv_ref[4 * part + k, 24:25, lanes]
            halves.append(row)
        return jnp.concatenate(halves + [jnp.full((6, LANES), -1.0, F32)], axis=0)

    codes = packed(slice(0, LANES)).astype(jnp.int32)
    ids = packed(slice(LANES, 256)).astype(jnp.int32)
    primal = gather_rows(
        codes,
        lambda a: slab_ref[a % 192 : a % 192 + 1, (a // 192) * LANES : (a // 192 + 1) * LANES],
        384,
    )
    store_digits(ids, high_ref, low_ref)
    for n, piece in enumerate(split_channels(primal, 3)):
        piece_ref[n] = piece
    partial = scatter_small(16, high_ref, low_ref, piece_ref, 2)
    for dest in range(out_ref.shape[0]):
        for c in range(3):
            start = 64 * c + 8 * dest
            out_ref[dest, 8 * c : 8 * c + 8, :] = slab_ref[start : start + 8, :]
        out_ref[dest, 24:32, 0:LANES] = partial[0:8, :]
        out_ref[dest, 24:32, LANES:] = jnp.zeros((8, LANES), F32)


def pick_kernel(
    recv_ref, idx_ref, small_ref, inv_hbm, out_ref, table_ref, pick_ref, inv_ref, mid_ref, prod_ref,
    lift_ref, sem,
):
    copy = pltpu.make_async_copy(inv_hbm, inv_ref, sem)
    copy.start()
    coarse = recv_ref[0, 24:32, 0:LANES]
    for src in range(1, recv_ref.shape[0]):
        coarse = coarse + recv_ref[src, 24:32, 0:LANES]
    for p in range(recv_ref.shape[0] // 2):
        for half in range(2):
            lanes = slice(half * LANES, (half + 1) * LANES)
            start = p * 48 + half * 24
            table_ref[start : start + 24, :] = (
                recv_ref[2 * p, 0:24, lanes] + recv_ref[2 * p + 1, 0:24, lanes]
            )
    table_rows = table_ref.shape[0]

    def block(t, carry):
        for sub in range(4):
            start = pl.multiple_of(t * 32 + sub * 8, 8)
            pick_ref[pl.ds(start, 8), :] = gather_rows(
                idx_ref[pl.ds(start, 8), :], lambda a: table_ref[a : a + 1, :], table_rows
            )
        return carry

    lax.fori_loop(0, 4, block, 0)
    mid_ref[...] = coarse
    copy.wait()
    coarse_rows = [jnp.broadcast_to(mid_ref[q : q + 1, :], (LANES, LANES)) for q in range(8)]
    ones = jnp.ones((8, LANES), F32)
    for part in range(8):
        rows = slice(part * LANES, (part + 1) * LANES)
        product = inv_ref[rows, 0:LANES] * coarse_rows[0]
        for q in range(1, 8):
            product = product + inv_ref[rows, q * LANES : (q + 1) * LANES] * coarse_rows[q]
        prod_ref[part] = product
        lift_ref[part : part + 1, :] = full_dot(ones, prod_ref[part], ((1,), (1,)))[0:1]
    lift = lift_ref[...]
    mine = own_lanes() == lax.rem(lax.axis_index("group"), 4)
    extra = jnp.where(mine, small_ref[0:2, :], 0.0)
    for h in range(pick_ref.shape[0] // 4):
        start = OWNER_ROWS * h
        out_ref[start : start + 8, :] = lift
        out_ref[start + 8 : start + 12, :] = pick_ref[4 * h : 4 * h + 4, :]
        out_ref[start + 12 : start + 14, :] = extra


def image_kernel(
    own_ref, pair_ref, dir_hbm, res_hbm, scale_hbm, iterate_hbm,
    image_ref, sums_ref, dir_ref, res_ref, scale_ref, iterate_ref,
    lift_ref, high_ref, low_ref, piece_ref, corr_ref, table_ref, sems,
):
    copies = start_copies(
        [
            (dir_hbm, dir_ref),
            (res_hbm, res_ref),
            (scale_hbm, scale_ref),
            (iterate_hbm, iterate_ref),
        ],
        sems,
    )
    groups = own_ref.shape[0] // OWNER_ROWS
    total = own_ref[0:8, :]
    for h in range(1, groups):
        total = total + own_ref[OWNER_ROWS * h : OWNER_ROWS * h + 8, :]
    lift_ref[...] = total

    def packed(row):
        rows = []
        for q in range(8):
            start = OWNER_ROWS * 4 * q + row
            value = own_ref[start : start + 1, :]
            for k in range(1, 4):
                start = OWNER_ROWS * (4 * q + k) + row
                value = value + own_ref[start : start + 1, :]
            rows.append(value)
        return jnp.concatenate(rows, axis=0).astype(jnp.int32)

    local = packed(12) - 512 * lax.axis_index("group")
    ids = packed(13)
    sender = 4 * lax.broadcasted_iota(jnp.int32, (8, LANES), 0) + jnp.broadcast_to(
        own_lanes(), (8, LANES)
    )
    valid = jnp.logical_and(local >= 0, local < 512)
    store_digits(jnp.where(valid, sender * 512 + local, -1), high_ref, low_ref)

    lifted = gather_rows(ids, lambda a: lift_ref[a : a + 1, :], 8)
    for n, piece in enumerate(split_channels(lifted, 3)):
        piece_ref[n] = piece
    corr_ref[...] = scatter_small(4 * groups, high_ref, low_ref, piece_ref, 8)
    for h in range(groups):
        start = OWNER_ROWS * h + 8
        table_ref[4 * h : 4 * h + 4, :] = (
            own_ref[start : start + 4, :] + corr_ref[4 * h : 4 * h + 4, :]
        )
    for copy in copies:
        copy.wait()

    half = dir_ref.shape[0]
    table_rows = 4 * groups

    def block(t, sums):
        sums = list(sums)
        for sub in range(2):
            start = pl.multiple_of(t * 16 + sub * 8, 8)
            plus, minus = (
                gather_rows(
                    pair_ref[pl.ds(base + start, 8), :],
                    lambda a: table_ref[a : a + 1, :],
                    table_rows,
                )
                for base in (0, half)
            )
            image = plus - minus
            image_ref[pl.ds(start, 8), :] = image
            res = res_ref[pl.ds(start, 8), :]
            scaled = scale_ref[pl.ds(start, 8), :]
            scaled_res = res * scaled
            sums[0] = sums[0] + scaled_res * res
            sums[1] = sums[1] + dir_ref[pl.ds(start, 8), :] * image
            sums[2] = sums[2] + scaled_res * image
            sums[3] = sums[3] + (scaled * image) * image
        return tuple(sums)

    zero = jnp.zeros((8, LANES), F32)
    sums = lax.fori_loop(0, half // 16, block, (zero, zero, zero, zero))
    lane = lax.broadcasted_iota(jnp.int32, (8, LANES), 1)
    packed_sums = jnp.zeros((8, LANES), F32)
    for n, part in enumerate(sums):
        value = jnp.sum(jnp.sum(part, axis=0, keepdims=True), axis=1, keepdims=True)
        packed_sums = jnp.where(lane == n, jnp.broadcast_to(value, (8, LANES)), packed_sums)
    for t in range(sums_ref.shape[0] // 8):
        sums_ref[8 * t : 8 * t + 8, :] = packed_sums


def update_kernel(
    sums_ref, dir_ref, res_ref, scale_ref, iterate_ref, image_ref, it_out, res_out, dir_out
):
    totals = jnp.sum(sums_ref[...], axis=0, keepdims=True)
    lane = lax.broadcasted_iota(jnp.int32, (1, LANES), 1)

    def pick(n):
        return jnp.sum(jnp.where(lane == n, totals, 0.0), axis=1, keepdims=True)

    old, curvature, cross, square = pick(0), pick(1), pick(2), pick(3)
    alpha = old / curvature
    new = old - 2.0 * alpha * cross + (alpha * alpha) * square
    beta = new / old
    direction = dir_ref[...]
    res_next = res_ref[...] - alpha * image_ref[...]
    it_out[...] = iterate_ref[...] + alpha * direction
    res_out[...] = res_next
    dir_out[...] = scale_ref[...] * res_next + beta * direction


def exchange(array, axis):
    return lax.all_to_all(array, axis, split_axis=0, concat_axis=0, tiled=True)


def f32(*shape):
    return jax.ShapeDtypeStruct(shape, F32)


def i32(*shape):
    return jax.ShapeDtypeStruct(shape, jnp.int32)


def body(
    mult_iterate,
    residual,
    direction,
    mult_scale,
    eigen_basis,
    eigen_values,
    elastic_coef,
    coarse_inverse,
    send_pos,
    pair_slots,
    prim_rows,
    coarse_idx,
):
    groups = lax.axis_size("group")
    pencils = lax.axis_size("pencil")
    iterate_now = mult_iterate.reshape(64, LANES)
    resid_now = residual.reshape(64, LANES)
    search_dir = direction.reshape(64, LANES)
    scale_now = mult_scale.reshape(64, LANES)
    cells = send_pos.reshape(128, LANES)
    pairs = pair_slots.reshape(2, 8192)
    primal = prim_rows.reshape(1, 32)
    coarse_ids = coarse_idx.reshape(1, 32)

    def resident(array):
        return pltpu.with_memory_space_constraint(array, pltpu.HBM)

    digits = [pltpu.VMEM((128, LANES), F32), pltpu.VMEM((128, LANES), F32)]
    pieces = pltpu.VMEM((2, 128, LANES), F32)
    small = [
        pltpu.VMEM((8, LANES), F32),
        pltpu.VMEM((8, LANES), F32),
        pltpu.VMEM((3, 8, LANES), F32),
    ]
    sources = (
        pairs,
        search_dir,
        cells,
        primal,
        coarse_ids,
        eigen_basis,
        eigen_values.transpose(1, 0, 2),
        elastic_coef.transpose(1, 0, 2),
    )
    back, pair_rows, cells, primals, *constants = call(
        back_kernel,
        (
            f32(128, LANES),
            i32(128, LANES),
            i32(128, LANES),
            f32(8, LANES),
            f32(128, 192),
            f32(192, 128),
            f32(256, 256),
            f32(256, 256),
            f32(6, 64, LANES),
        ),
        [HBM] * len(sources),
        "back",
        [
            pltpu.VMEM((2, 8192), jnp.int32),
            pltpu.VMEM((64, LANES), F32),
            pltpu.VMEM((1, 32), jnp.int32),
            pltpu.VMEM((1, 32), jnp.int32),
            pltpu.VMEM((3, 64, 64), F32),
            pltpu.VMEM((3, 4, 64), F32),
            pltpu.VMEM((3, 4, 3), F32),
        ]
        + digits
        + [pieces, pltpu.SemaphoreType.DMA((len(sources),))],
    )(*(resident(source) for source in sources))
    arrived = exchange(back.reshape(groups, 4, LANES), "group").reshape(128, LANES)

    loads, slots = call(
        load_kernel,
        (f32(pencils, 32, 256), i32(128, LANES)),
        [VMEM] * 3,
        "load",
        digits + [pieces, pltpu.VMEM((192, LANES), F32)],
    )(arrived, cells, primals)
    columns = exchange(loads, "pencil")

    partial = call(
        solve_kernel,
        f32(pencils, 32, 256),
        [VMEM] * 6,
        "solve",
        [
            pltpu.VMEM((256, LANES), F32),
            pltpu.VMEM((64, 8, LANES), F32),
            pltpu.VMEM((64, 8, LANES), F32),
            pltpu.VMEM((192, 256), F32),
        ]
        + small,
    )(columns, *constants)
    slabs = exchange(partial, "pencil")

    picked = call(
        pick_kernel,
        f32(groups * OWNER_ROWS, LANES),
        [VMEM, VMEM, VMEM, HBM],
        "pick",
        [
            pltpu.VMEM((192, LANES), F32),
            pltpu.VMEM((128, LANES), F32),
            pltpu.VMEM((1024, 1024), F32),
            pltpu.VMEM((8, LANES), F32),
            pltpu.VMEM((8, LANES, LANES), F32),
            pltpu.VMEM((8, LANES), F32),
            pltpu.SemaphoreType.DMA,
        ],
    )(slabs, slots, primals, resident(coarse_inverse))
    owner = exchange(picked.reshape(groups, 1, OWNER_ROWS * LANES), "group")

    shape = f32(64, LANES)
    image, sums, *vectors = call(
        image_kernel,
        (shape, f32(groups * pencils, LANES), shape, shape, shape, shape),
        [VMEM, VMEM] + [HBM] * 4,
        "image",
        [pltpu.VMEM((8, LANES), F32)]
        + small
        + [
            pltpu.VMEM((128, LANES), F32),
            pltpu.VMEM((128, LANES), F32),
            pltpu.SemaphoreType.DMA((4,)),
        ],
    )(
        owner.reshape(groups * OWNER_ROWS, LANES),
        pair_rows,
        *(resident(array) for array in (search_dir, resid_now, scale_now, iterate_now)),
    )
    totals = exchange(sums, ("group", "pencil"))

    outs = call(update_kernel, (shape, shape, shape), [VMEM] * 6, "update")(
        totals, *vectors, image
    )
    return tuple(out.reshape(1, 1, -1) for out in outs)


def solution(mesh):
    in_specs = (
        P("group", "pencil", None),
        P("group", "pencil", None),
        P("group", "pencil", None),
        P("group", "pencil", None),
        P("group", None, None, None),
        P("group", None, None),
        P("group", None, None),
        P(),
        P("group", "pencil", None),
        P("group", "pencil", None, None),
        P("group", "pencil", None),
        P("group", "pencil", None),
    )
    out_specs = (P("group", "pencil", None), P("group", "pencil", None), P("group", "pencil", None))
    return jax.shard_map(body, mesh=mesh, in_specs=in_specs, out_specs=out_specs, check_vma=False)
```

time: 881 us -> 98.4 us (0.11)
  local copies, waits for them, and re-layouts: 521 us -> 0 us
  blocking collectives: 220 us -> 76.8 us
  waiting for transfers between devices: 54.7 us -> 0 us
  matrix products: 33.9 us -> 0 us
  starting transfers between devices: 28.2 us -> 0 us
  Pallas kernels: 0 us -> 20.6 us
  other arithmetic: 14.1 us -> 0 us
    gather x4 -> x0, local copies, waits for them, and re-layouts: 253 us -> none  [the longest x1 160 us: apply_inverse(): return volume_to_cycle(displace).reshape(-1)[positions]]
    psum x3 -> x0, blocking collectives: 220 us -> none  [the longest x1 74 us: body(): norm_next = lax.psum(jnp.sum(resid_next * precond), ('group', 'pencil'))]
    scatter x3 -> x0, local copies, waits for them, and re-layouts: 124 us -> none  [the longest x2 63.2 us: body(): back_rows = jnp.zeros((rows_count,), jnp.float32).at[pair_rows[0]].set(se...]
    all_to_all x0 -> x5, blocking collectives: none -> 76.8 us  [exchange(): return lax.all_to_all(array, axis, split_axis=0, concat_axis=0, tiled=True)]
    unnamed x40 -> x0, local copies, waits for them, and re-layouts: 70.6 us -> none
    all_to_all x4 -> x0, waiting for transfers between devices: 54.7 us -> none  [the longest x1 19.3 us: apply_inverse(): lax.all_to_all(mixed, 'pencil', split_axis=0, concat_axis=3, tiled=True)]
    reshape x5 -> x0, local copies, waits for them, and re-layouts: 44 us -> none  [the longest x1 34.6 us: apply_inverse(): partial_yz.reshape(slab_x, patches, components, extent * extent)]
    dot_general x9 -> x0, matrix products: 33.9 us -> none  [the longest x1 5.64 us: body(): lifted = jnp.dot(coarse_inverse, total_coarse, precision=highest)]
  transfers between devices with their start and end apart: 4 -> 0, of which waited for: 4 -> 0; matrix products, arithmetic and copies ran while one was open for 0% -> 0% of each run, Pallas kernels for 0% -> 0%
where the time goes in v2:
time: 98.4 us; the launch traced here: 98 us
  blocking collectives  76.8 us (78%)
  Pallas kernels  20.6 us (21%)
    all_to_all x5, blocking collectives, exchange(): return lax.all_to_all(array, axis, split_axis=0, concat_axis=0, tiled=True)  76.8 us
    pallas_call x1, Pallas kernels, body(): call(pick_kernel, f32(groups * OWNER_ROWS, LANES), [VMEM, VMEM, VMEM, HBM...  4.62 us
    pallas_call x1, Pallas kernels, body(): call(back_kernel, (f32(128, LANES), i32(128, LANES), i32(128, LANES), f32...  4.33 us
    pallas_call x1, Pallas kernels, body(): call(solve_kernel, f32(pencils, 32, 256), [VMEM] * 6, 'solve', [pltpu.VME...  4.04 us
    pallas_call x1, Pallas kernels, body(): call(image_kernel, (shape, f32(groups * pencils, LANES), shape, shape, sh...  3.45 us
    pallas_call x1, Pallas kernels, body(): call(load_kernel, (f32(pencils, 32, 256), i32(128, LANES)), [VMEM] * 3, '...  3.37 us

profile of v2, /device:TPU:1, one launch (start us, length us, event | category | flops | bytes accessed | tf_op | source)
XLA Modules:
  0.0 98.0 jit_solution(16236945147470411500)
XLA Ops:
  0.6 4.3 %back.1 = (f32[128,128]{1,0:T(8,128)S(1)}, s32[128,128]{1,0:T(8,128)S(1)}, s32[128,128]{1,0:T(8,128)S(1)}, f32[8,128]{1,0:T(8,128)S(1)}, f32[128,192]{1,0:T(8,12...) custom-call(s32[2,8192]{1,0:T(2,128)} %bitcast.29, ...), custom_call_target="tpu_custom_call" | custom-call | flops 4000000 | bytes 262144 | tf_op jit(solution)/shard_map/back/pallas_call | solution.py:580
  5.0 20.7 %all_to_all.31 = f32[32,4,128]{2,1,0:T(4,128)S(1)} all-to-all(f32[32,4,128]{2,1,0:T(4,128)S(1)} %bitcast.26), channel_id=1, replica_groups=mesh['group'=32,'pencil'=8] {'group'}, dimensions={0} | all-to-all | bytes 131072 | tf_op jit(solution)/shard_map/all_to_all | solution.py:524
  25.6 3.4 %load.1 = (f32[8,32,256]{2,1,0:T(8,128)S(1)}, s32[128,128]{1,0:T(8,128)S(1)}) custom-call(f32[128,128]{1,0:T(8,128)S(1)} %bitcast.24, s32[128,128]{1,0:T(8,128)S(1)} %get-tuple-element.24.pos_ref, f32[8,128]{1,0:T(8,128)S(1)} %get-tuple-element.25.small_ref), custom_call_target="tpu_custom_call" | custom-call | flops 4000000 | bytes 262144 | tf_op jit(solution)/shard_map/load/pallas_call | solution.py:609
  29.0 12.7 %all_to_all.32.recv_ref = f32[8,32,256]{2,1,0:T(8,128)S(1)} all-to-all(f32[8,32,256]{2,1,0:T(8,128)S(1)} %get-tuple-element.26), channel_id=1, replica_groups=mesh['group'=32,'pencil'=8] {'pencil'}, dimensions={0} | all-to-all | bytes 524288 | tf_op jit(solution)/shard_map/all_to_all | solution.py:524
  41.7 4.0 %solve.1 = f32[8,32,256]{2,1,0:T(8,128)S(1)} custom-call(f32[8,32,256]{2,1,0:T(8,128)S(1)} %all_to_all.32.recv_ref, f32[128,192]{1,0:T(8,128)S(1)} %get-tuple-element.27.bxt_ref, f32[192,128]{1,0:T(8,128)S(1)} %get-tuple-element.28.bx_ref, f32[256,256]{1,0:T(8,128)S(1)} %get-tuple-element.29.bdt_ref, f32[256,256]{1,0:T(8,128)S(1)} %get-tuple-element.30.bd_ref, ...), custom_call_target="tpu_custom_call" | custom-call | flops 4000000 | bytes 262144 | tf_op jit(solution)/shard_map/solve/pallas_call | solution.py:618
  45.8 9.9 %all_to_all.33.recv_ref = f32[8,32,256]{2,1,0:T(8,128)S(1)} all-to-all(f32[8,32,256]{2,1,0:T(8,128)S(1)} %solve.1), channel_id=1, replica_groups=mesh['group'=32,'pencil'=8] {'pencil'}, dimensions={0} | all-to-all | bytes 524288 | tf_op jit(solution)/shard_map/all_to_all | solution.py:524
  55.7 4.6 %pick.1 = f32[448,128]{1,0:T(8,128)S(1)} custom-call(f32[8,32,256]{2,1,0:T(8,128)S(1)} %all_to_all.33.recv_ref, s32[128,128]{1,0:T(8,128)S(1)} %get-tuple-element.32.idx_ref, f32[8,128]{1,0:T(8,128)S(1)} %get-tuple-element.25.small_ref, f32[1024,1024]{1,0:T(8,128)} %inv_hbm.1), custom_call_target="tpu_custom_call" | custom-call | flops 4000000 | bytes 262144 | tf_op jit(solution)/shard_map/pick/pallas_call | solution.py:633
  60.3 12.6 %all_to_all.34 = f32[32,1,1792]{2,1,0:T(1,128)S(1)} all-to-all(f32[32,1,1792]{2,1,0:T(1,128)S(1)} %bitcast.22), channel_id=1, replica_groups=mesh['group'=32,'pencil'=8] {'group'}, dimensions={0} | all-to-all | bytes 458752 | tf_op jit(solution)/shard_map/all_to_all | solution.py:524
  72.9 3.4 %image.1 = (f32[64,128]{1,0:T(8,128)S(1)}, f32[256,128]{1,0:T(8,128)S(1)}, f32[64,128]{1,0:T(8,128)S(1)}, f32[64,128]{1,0:T(8,128)S(1)}, f32[64,128]{1,0:T(8,128)S(1)}, /*index=5*/f32[64,128]{1,0:T(8,128)S(1)}) custom-call(f32[448,128]{1,0:T(8,128)S(1)} %bitcast.21, s32[128,128]{1,0:T(8,128)S(1)} %get-tuple-element.33.pair_ref, f32[64,128]{1,0:T(8,128)} %bitcast.28, ...), custom_call_target="tpu_custom_call" | custom-call | flops 4000000 | bytes 262144 | tf_op jit(solution)/shard_map/image/pallas_call | solution.py:651
  76.3 20.9 %all_to_all.35 = f32[256,1,128]{2,1,0:T(1,128)S(1)} all-to-all(f32[256,1,128]{2,1,0:T(1,128)S(1)} %bitcast.25), channel_id=1, replica_groups=mesh['group'=32,'pencil'=8] {'group','pencil'}, dimensions={0} | all-to-all | bytes 262144 | tf_op jit(solution)/shard_map/all_to_all | solution.py:524
  97.3 0.8 update.1

commit v3 on v2

--- a/solution.py
+++ b/solution.py
@@ -137,7 +137,10 @@
     return jnp.concatenate([row] * 4, axis=1)
 
 
-CHUNK = 32
+CHUNK = 64
+WIDE = 192
+LOAD_ROWS = 34
+SLAB_ROWS = 40
 OWNER_ROWS = 14
 
 
@@ -155,7 +158,7 @@
     pair_hbm, dir_hbm, cells_hbm, prim_hbm, ids_hbm, basis_hbm, values_hbm, coeff_hbm,
     out_ref, idx_ref, cells_ref, small_ref, bxt_ref, bx_ref, bdt_ref, bd_ref, cst_ref,
     pair_ref, dir_ref, prim_ref, ids_ref, basis_ref, values_ref, coeff_ref,
-    high_ref, low_ref, piece_ref, sems,
+    high_ref, low_ref, piece_ref, acc_ref, sems,
 ):
     pencil = lax.axis_index("pencil")
     patch = lax.div(pencil, 2)
@@ -174,10 +177,8 @@
         sems,
     )
     half = dir_ref.shape[0]
-    bx_ref[...] = jnp.zeros(bx_ref.shape, F32)
-    bxt_ref[...] = jnp.zeros(bxt_ref.shape, F32)
-    bd_ref[...] = jnp.zeros(bd_ref.shape, F32)
-    bdt_ref[...] = jnp.zeros(bdt_ref.shape, F32)
+    for ref in (bx_ref, bxt_ref, bd_ref, bdt_ref):
+        ref[...] = jnp.zeros(ref.shape, BF16)
     copies[0].wait()
     copies[1].wait()
     for k in range(half):
@@ -188,14 +189,15 @@
     for n, piece in enumerate(split_channels(dir_ref[...], 2)):
         piece_ref[n, :half, :] = piece
         piece_ref[n, half:, :] = -piece
-    out_ref[...] = scatter_large(
-        2 * half,
+    acc_ref[...] = scatter_large(
+        WIDE,
         high_ref,
         low_ref,
         lambda n, t, r: piece_ref[n, pl.ds(t * CHUNK + r, 1), :],
         2 * half,
         CHUNK,
     )
+    out_ref[...] = acc_ref[: 2 * half, :]
     for copy in copies[2:]:
         copy.wait()
     small_ref[...] = jnp.zeros(small_ref.shape, F32)
@@ -208,15 +210,12 @@
     half_x = jnp.where(side == 1, along_x[:, 32:64], along_x[:, 0:32])
     flipped = full_dot(identity, along_x, ((1,), (1,)))
     half_flipped = jnp.where(side == 1, flipped[32:64], flipped[0:32])
-    for c in range(3):
-        bx_ref[64 * c : 64 * c + 64, 32 * c : 32 * c + 32] = half_x
-        bxt_ref[32 * c : 32 * c + 32, 64 * c : 64 * c + 64] = half_flipped
     flipped_y = full_dot(identity, along_y, ((1,), (1,)))
     flipped_z = full_dot(identity, along_z, ((1,), (1,)))
-    for block in range(4):
-        part = slice(64 * block, 64 * block + 64)
-        bd_ref[part, part] = along_z if block in (0, 3) else along_y
-        bdt_ref[part, part] = flipped_z if block in (0, 3) else flipped_y
+    store_left(bx_ref, 128, [(0, 0, along_x), (64, 64, half_x)])
+    store_left(bxt_ref, 128, [(0, 0, flipped), (64, 64, half_flipped)])
+    store_left(bd_ref, 256, diagonal(along_z, along_y))
+    store_left(bdt_ref, 256, diagonal(flipped_z, flipped_y))
 
     def spread(column):
         return jnp.broadcast_to(column, (64, LANES))
@@ -228,16 +227,19 @@
     lane = lax.broadcasted_iota(jnp.int32, (1, LANES), 1)
 
     def weight(dim):
-        value = jnp.zeros((1, LANES), F32)
-        for c in range(3):
-            here = lax.shift_right_logical(lane, 5) == c
-            coeff = coeff_ref[c, pl.ds(patch, 1), :][:, dim : dim + 1]
-            value = jnp.where(here, jnp.broadcast_to(coeff, (1, LANES)), value)
-        return value
+        own = jnp.where(
+            side == 1, coeff_ref[2, pl.ds(patch, 1), :], coeff_ref[0, pl.ds(patch, 1), :]
+        )
+        shared = coeff_ref[1, pl.ds(patch, 1), :]
+        own, shared = (
+            jnp.broadcast_to(value[:, dim : dim + 1], (1, LANES)) for value in (own, shared)
+        )
+        return jnp.where(lane < 64, own, jnp.where(lane < 96, shared, 0.0))
 
     x_values, y_values, z_values = (values_ref[dim, pl.ds(patch, 1), :] for dim in range(3))
     half_values = jnp.where(side == 1, x_values[:, 32:64], x_values[:, 0:32])
-    x_term = jnp.where(lane >= 96, 1.0, weight(0) * spread_lanes(half_values))
+    lane_values = jnp.concatenate([x_values, half_values, half_values], axis=1)
+    x_term = jnp.where(lane >= 96, 1.0, weight(0) * lane_values)
     y_term = weight(1) * spread(column_of(y_values))
     cst_ref[4] = x_term + y_term
     cst_ref[5] = weight(2) * spread(column_of(z_values))
@@ -267,22 +269,56 @@
     primal = jnp.broadcast_to(small_ref[0:1, :], (8, LANES)).astype(jnp.int32)
     cells = gather_rows(primal, lambda a: pos_ref[a : a + 1, :].astype(F32), rows)
     patch, component, along_x, half, lane = cell_digits(cells[0:1])
-    place = half * 192.0 + component * 64.0 + along_x + (8 * pencil).astype(F32)
+    place = half * 128.0 + along_x + (8 * pencil).astype(F32)
     code = place * 128.0 + lane
     ids = jnp.where(mine, small_ref[1:2, :], 0.0)
-    for dest in range(out_ref.shape[0]):
+    for dest in range(out_ref.shape[0] // LOAD_ROWS):
+        base = LOAD_ROWS * dest
+        own = 2 * (dest % 2)
         for side in range(2):
             start = (dest // 2) * 48 + side * 24
-            out_ref[dest, 0:24, side * LANES : (side + 1) * LANES] = acc_ref[start : start + 24, :]
-        own = jnp.where(patch == float(dest // 2), code, -1.0)
-        out_ref[dest, 24:32, :] = jnp.zeros((8, 256), F32)
-        out_ref[dest, 24:25, 0:LANES] = jnp.where(mine, own, 0.0)
-        out_ref[dest, 24:25, LANES:] = ids
+            for n, c in enumerate((own, 1)):
+                out_ref[base + side * 16 + 8 * n : base + side * 16 + 8 * n + 8, :] = acc_ref[
+                    start + 8 * c : start + 8 * c + 8, :
+                ]
+        here = jnp.where(
+            component == float(own), code, jnp.where(component == 1.0, code + 8192.0, -1.0)
+        )
+        here = jnp.where(patch == float(dest // 2), here, -1.0)
+        out_ref[base + 32 : base + 33, :] = jnp.where(mine, here, 0.0)
+        out_ref[base + 33 : base + 34, :] = ids
 
 
 def full_dot(left, right, contract):
     return lax.dot_general(
         left, right, ((contract[0], contract[1]), ((), ())), precision=HIGHEST,
+        preferred_element_type=F32,
+    )
+
+
+def split_pair(value):
+    high = value.astype(BF16)
+    return high, (value - high.astype(F32)).astype(BF16)
+
+
+def store_left(ref, width, blocks):
+    for row, lane, block in blocks:
+        high, low = split_pair(block)
+        for n, piece in enumerate((high, high, low)):
+            start = n * width + lane
+            ref[row : row + block.shape[0], start : start + block.shape[1]] = piece
+
+
+def diagonal(outer, inner):
+    return [(64 * n, 64 * n, block) for n, block in enumerate((outer, inner, inner, outer))]
+
+
+def split_dot(left_ref, right, contract_right):
+    high, low = split_pair(right)
+    return lax.dot_general(
+        left_ref[...],
+        jnp.concatenate([high, low, high], axis=contract_right),
+        (((1,), (contract_right,)), ((), ())),
         preferred_element_type=F32,
     )
 
@@ -299,12 +335,22 @@
     recv_ref, bxt_ref, bx_ref, bdt_ref, bd_ref, cst_ref, out_ref, fwd_ref, d0_ref, d1_ref,
     slab_ref, high_ref, low_ref, piece_ref,
 ):
-    sources = recv_ref.shape[0]
+    sources = recv_ref.shape[0] // LOAD_ROWS
     load = jnp.concatenate(
-        [recv_ref[src, 8 * c : 8 * c + 8, :] for c in range(3) for src in range(sources)], axis=0
-    )
-    along_x = full_dot(bxt_ref[...], load, ((1,), (0,)))
-    fwd_ref[...] = full_dot(bdt_ref[...], along_x, ((1,), (1,)))
+        [
+            jnp.concatenate(
+                [
+                    recv_ref[LOAD_ROWS * src + start : LOAD_ROWS * src + start + 8, :]
+                    for start in (8 * n, 16 + 8 * n)
+                ],
+                axis=1,
+            )
+            for n in range(2)
+            for src in range(sources)
+        ],
+        axis=0,
+    )
+    fwd_ref[...] = split_dot(bdt_ref, split_dot(bxt_ref, load, 0), 1)
 
     def step(j, carry):
         top, bottom = carry
@@ -333,53 +379,63 @@
     edges = jnp.concatenate(
         [top, jnp.sum(d0_ref[...], axis=1), jnp.sum(d1_ref[...], axis=1), bottom], axis=0
     )
-    cells = full_dot(bd_ref[...], edges, ((1,), (0,)))
-    slab_ref[...] = full_dot(bx_ref[...], cells, ((1,), (1,)))
-
-    def packed(lanes):
+    slab_ref[...] = split_dot(bx_ref, split_dot(bd_ref, edges, 0), 1)
+
+    def packed(row):
         halves = []
         for part in range(2):
-            row = recv_ref[4 * part, 24:25, lanes]
-            for k in range(1, 4):
-                row = row + recv_ref[4 * part + k, 24:25, lanes]
-            halves.append(row)
+            starts = [LOAD_ROWS * (4 * part + k) + row for k in range(4)]
+            value = recv_ref[starts[0] : starts[0] + 1, :]
+            for start in starts[1:]:
+                value = value + recv_ref[start : start + 1, :]
+            halves.append(value)
         return jnp.concatenate(halves + [jnp.full((6, LANES), -1.0, F32)], axis=0)
 
-    codes = packed(slice(0, LANES)).astype(jnp.int32)
-    ids = packed(slice(LANES, 256)).astype(jnp.int32)
+    codes = packed(32).astype(jnp.int32)
+    ids = packed(33).astype(jnp.int32)
     primal = gather_rows(
         codes,
-        lambda a: slab_ref[a % 192 : a % 192 + 1, (a // 192) * LANES : (a // 192 + 1) * LANES],
-        384,
+        lambda a: slab_ref[a % 128 : a % 128 + 1, (a // 128) * LANES : (a // 128 + 1) * LANES],
+        256,
     )
     store_digits(ids, high_ref, low_ref)
     for n, piece in enumerate(split_channels(primal, 3)):
         piece_ref[n] = piece
     partial = scatter_small(16, high_ref, low_ref, piece_ref, 2)
-    for dest in range(out_ref.shape[0]):
-        for c in range(3):
-            start = 64 * c + 8 * dest
-            out_ref[dest, 8 * c : 8 * c + 8, :] = slab_ref[start : start + 8, :]
-        out_ref[dest, 24:32, 0:LANES] = partial[0:8, :]
-        out_ref[dest, 24:32, LANES:] = jnp.zeros((8, LANES), F32)
+    for dest in range(out_ref.shape[0] // SLAB_ROWS):
+        base = SLAB_ROWS * dest
+        for half in range(2):
+            lanes = slice(half * LANES, (half + 1) * LANES)
+            for n in range(2):
+                start = base + 16 * half + 8 * n
+                out_ref[start : start + 8, :] = slab_ref[
+                    64 * n + 8 * dest : 64 * n + 8 * dest + 8, lanes
+                ]
+        out_ref[base + 32 : base + 40, :] = partial[0:8, :]
 
 
 def pick_kernel(
-    recv_ref, idx_ref, small_ref, inv_hbm, out_ref, table_ref, pick_ref, inv_ref, mid_ref, prod_ref,
+    recv_ref, idx_ref, small_ref, inv_hbm, out_ref, table_ref, pick_ref, inv_ref, mid_ref,
     lift_ref, sem,
 ):
     copy = pltpu.make_async_copy(inv_hbm, inv_ref, sem)
     copy.start()
-    coarse = recv_ref[0, 24:32, 0:LANES]
-    for src in range(1, recv_ref.shape[0]):
-        coarse = coarse + recv_ref[src, 24:32, 0:LANES]
-    for p in range(recv_ref.shape[0] // 2):
+    sources = recv_ref.shape[0] // SLAB_ROWS
+
+    def block_of(src, start):
+        return recv_ref[SLAB_ROWS * src + start : SLAB_ROWS * src + start + 8, :]
+
+    coarse = block_of(0, 32)
+    for src in range(1, sources):
+        coarse = coarse + block_of(src, 32)
+    for p in range(sources // 2):
         for half in range(2):
-            lanes = slice(half * LANES, (half + 1) * LANES)
             start = p * 48 + half * 24
-            table_ref[start : start + 24, :] = (
-                recv_ref[2 * p, 0:24, lanes] + recv_ref[2 * p + 1, 0:24, lanes]
+            table_ref[start : start + 8, :] = block_of(2 * p, 16 * half)
+            table_ref[start + 8 : start + 16, :] = block_of(2 * p, 16 * half + 8) + block_of(
+                2 * p + 1, 16 * half + 8
             )
+            table_ref[start + 16 : start + 24, :] = block_of(2 * p + 1, 16 * half)
     table_rows = table_ref.shape[0]
 
     def block(t, carry):
@@ -394,14 +450,14 @@
     mid_ref[...] = coarse
     copy.wait()
     coarse_rows = [jnp.broadcast_to(mid_ref[q : q + 1, :], (LANES, LANES)) for q in range(8)]
-    ones = jnp.ones((8, LANES), F32)
+    ones = jnp.ones((16, LANES), BF16)
     for part in range(8):
         rows = slice(part * LANES, (part + 1) * LANES)
         product = inv_ref[rows, 0:LANES] * coarse_rows[0]
         for q in range(1, 8):
             product = product + inv_ref[rows, q * LANES : (q + 1) * LANES] * coarse_rows[q]
-        prod_ref[part] = product
-        lift_ref[part : part + 1, :] = full_dot(ones, prod_ref[part], ((1,), (1,)))[0:1]
+        high, low = split_pair(product)
+        lift_ref[part : part + 1, :] = (pair_dot(ones, high) + pair_dot(ones, low))[0:1]
     lift = lift_ref[...]
     mine = own_lanes() == lax.rem(lax.axis_index("group"), 4)
     extra = jnp.where(mine, small_ref[0:2, :], 0.0)
@@ -584,10 +640,10 @@
             i32(128, LANES),
             i32(128, LANES),
             f32(8, LANES),
-            f32(128, 192),
-            f32(192, 128),
-            f32(256, 256),
-            f32(256, 256),
+            jax.ShapeDtypeStruct((128, 384), BF16),
+            jax.ShapeDtypeStruct((128, 384), BF16),
+            jax.ShapeDtypeStruct((256, 768), BF16),
+            jax.ShapeDtypeStruct((256, 768), BF16),
             f32(6, 64, LANES),
         ),
         [HBM] * len(sources),
@@ -602,33 +658,33 @@
             pltpu.VMEM((3, 4, 3), F32),
         ]
         + digits
-        + [pieces, pltpu.SemaphoreType.DMA((len(sources),))],
+        + [pieces, pltpu.VMEM((WIDE, LANES), F32), pltpu.SemaphoreType.DMA((len(sources),))],
     )(*(resident(source) for source in sources))
     arrived = exchange(back.reshape(groups, 4, LANES), "group").reshape(128, LANES)
 
     loads, slots = call(
         load_kernel,
-        (f32(pencils, 32, 256), i32(128, LANES)),
+        (f32(pencils * LOAD_ROWS, LANES), i32(128, LANES)),
         [VMEM] * 3,
         "load",
         digits + [pieces, pltpu.VMEM((192, LANES), F32)],
     )(arrived, cells, primals)
-    columns = exchange(loads, "pencil")
+    columns = exchange(loads.reshape(pencils, 1, LOAD_ROWS * LANES), "pencil")
 
     partial = call(
         solve_kernel,
-        f32(pencils, 32, 256),
+        f32(pencils * SLAB_ROWS, LANES),
         [VMEM] * 6,
         "solve",
         [
             pltpu.VMEM((256, LANES), F32),
             pltpu.VMEM((64, 8, LANES), F32),
             pltpu.VMEM((64, 8, LANES), F32),
-            pltpu.VMEM((192, 256), F32),
+            pltpu.VMEM((128, 256), F32),
         ]
         + small,
-    )(columns, *constants)
-    slabs = exchange(partial, "pencil")
+    )(columns.reshape(pencils * LOAD_ROWS, LANES), *constants)
+    slabs = exchange(partial.reshape(pencils, 1, SLAB_ROWS * LANES), "pencil")
 
     picked = call(
         pick_kernel,
@@ -640,11 +696,10 @@
             pltpu.VMEM((128, LANES), F32),
             pltpu.VMEM((1024, 1024), F32),
             pltpu.VMEM((8, LANES), F32),
-            pltpu.VMEM((8, LANES, LANES), F32),
             pltpu.VMEM((8, LANES), F32),
             pltpu.SemaphoreType.DMA,
         ],
-    )(slabs, slots, primals, resident(coarse_inverse))
+    )(slabs.reshape(pencils * SLAB_ROWS, LANES), slots, primals, resident(coarse_inverse))
     owner = exchange(picked.reshape(groups, 1, OWNER_ROWS * LANES), "group")
 
     shape = f32(64, LANES)

time: 98.4 us -> 94.1 us (0.956)
  blocking collectives: 76.8 us -> 74.6 us
  Pallas kernels: 20.6 us -> 18.5 us
    all_to_all x5, blocking collectives: 76.8 us -> 74.6 us  [exchange(): return lax.all_to_all(array, axis, split_axis=0, concat_axis=0, tiled=True)]
    pallas_call x2, Pallas kernels: 7.41 us -> 6.08 us  [the longest x1 3.13 us: body(): call(solve_kernel, f32(pencils * SLAB_ROWS, LANES), [VMEM] * 6, 'solve',...]
where the time goes in v3:
time: 94.1 us; the launch traced here: 93.7 us
  blocking collectives  74.6 us (79%)
  Pallas kernels  18.5 us (20%)
    all_to_all x5, blocking collectives, exchange(): return lax.all_to_all(array, axis, split_axis=0, concat_axis=0, tiled=True)  74.6 us
    pallas_call x1, Pallas kernels, body(): call(back_kernel, (f32(128, LANES), i32(128, LANES), i32(128, LANES), f32...  4.09 us
    pallas_call x1, Pallas kernels, body(): call(pick_kernel, f32(groups * OWNER_ROWS, LANES), [VMEM, VMEM, VMEM, HBM...  4.08 us
    pallas_call x1, Pallas kernels, body(): call(image_kernel, (shape, f32(groups * pencils, LANES), shape, shape, sh...  3.45 us
    pallas_call x1, Pallas kernels, body(): call(solve_kernel, f32(pencils * SLAB_ROWS, LANES), [VMEM] * 6, 'solve',...  3.13 us
    pallas_call x1, Pallas kernels, body(): call(load_kernel, (f32(pencils * LOAD_ROWS, LANES), i32(128, LANES)), [VM...  2.95 us

profile of v3, /device:TPU:1, one launch (start us, length us, event | category | flops | bytes accessed | tf_op | source)
XLA Modules:
  0.0 93.7 jit_solution(7467781089012960273)
XLA Ops:
  0.6 4.1 %back.1 = (f32[128,128]{1,0:T(8,128)S(1)}, s32[128,128]{1,0:T(8,128)S(1)}, s32[128,128]{1,0:T(8,128)S(1)}, f32[8,128]{1,0:T(8,128)S(1)}, bf16[128,384]{1,0:T(8,1...) custom-call(s32[2,8192]{1,0:T(2,128)} %bitcast.37, ...), custom_call_target="tpu_custom_call" | custom-call | flops 4000000 | bytes 262144 | tf_op jit(solution)/shard_map/back/pallas_call | solution.py:636
  4.7 20.7 %all_to_all.31 = f32[32,4,128]{2,1,0:T(4,128)S(1)} all-to-all(f32[32,4,128]{2,1,0:T(4,128)S(1)} %bitcast.34), channel_id=1, replica_groups=mesh['group'=32,'pencil'=8] {'group'}, dimensions={0} | all-to-all | bytes 131072 | tf_op jit(solution)/shard_map/all_to_all | solution.py:580
  25.4 3.0 %load.1 = (f32[272,128]{1,0:T(8,128)S(1)}, s32[128,128]{1,0:T(8,128)S(1)}) custom-call(f32[128,128]{1,0:T(8,128)S(1)} %bitcast.31, s32[128,128]{1,0:T(8,128)S(1)} %get-tuple-element.24.pos_ref, f32[8,128]{1,0:T(8,128)S(1)} %get-tuple-element.25.small_ref), custom_call_target="tpu_custom_call" | custom-call | flops 4000000 | bytes 262144 | tf_op jit(solution)/shard_map/load/pallas_call | solution.py:665
  28.4 11.5 %all_to_all.32 = f32[8,1,4352]{2,1,0:T(1,128)S(1)} all-to-all(f32[8,1,4352]{2,1,0:T(1,128)S(1)} %bitcast.32), channel_id=1, replica_groups=mesh['group'=32,'pencil'=8] {'pencil'}, dimensions={0} | all-to-all | bytes 278528 | tf_op jit(solution)/shard_map/all_to_all | solution.py:580
  39.9 3.1 %solve.1 = f32[320,128]{1,0:T(8,128)S(1)} custom-call(f32[272,128]{1,0:T(8,128)S(1)} %bitcast.29, bf16[128,384]{1,0:T(8,128)(2,1)S(1)} %get-tuple-element.27.bxt_ref, bf16[128,384]{1,0:T(8,128)(2,1)S(1)} %get-tuple-element.28.bx_ref, bf16[256,768]{1,0:T(8,128)(2,1)S(1)} %get-tuple-element.29.bdt_ref, bf16[256,768]{1,0:T(8,128)(2,1)S(1)} %get-tuple-element.30.bd_ref, ...), custom_call_target="tpu_custom_call" | custom-call | flops 4000000 | bytes 262144 | tf_op jit(solution)/shard_map/solve/pallas_call | solution.py:674
  43.0 8.9 %all_to_all.33 = f32[8,1,5120]{2,1,0:T(1,128)S(1)} all-to-all(f32[8,1,5120]{2,1,0:T(1,128)S(1)} %bitcast.27), channel_id=1, replica_groups=mesh['group'=32,'pencil'=8] {'pencil'}, dimensions={0} | all-to-all | bytes 327680 | tf_op jit(solution)/shard_map/all_to_all | solution.py:580
  51.9 4.1 %pick.1 = f32[448,128]{1,0:T(8,128)S(1)} custom-call(f32[320,128]{1,0:T(8,128)S(1)} %bitcast.28, s32[128,128]{1,0:T(8,128)S(1)} %get-tuple-element.32.idx_ref, f32[8,128]{1,0:T(8,128)S(1)} %get-tuple-element.25.small_ref, f32[1024,1024]{1,0:T(8,128)} %inv_hbm.1), custom_call_target="tpu_custom_call" | custom-call | flops 4000000 | bytes 262144 | tf_op jit(solution)/shard_map/pick/pallas_call | solution.py:689
  56.0 12.5 %all_to_all.34 = f32[32,1,1792]{2,1,0:T(1,128)S(1)} all-to-all(f32[32,1,1792]{2,1,0:T(1,128)S(1)} %bitcast.26), channel_id=1, replica_groups=mesh['group'=32,'pencil'=8] {'group'}, dimensions={0} | all-to-all | bytes 458752 | tf_op jit(solution)/shard_map/all_to_all | solution.py:580
  68.5 3.4 %image.1 = (f32[64,128]{1,0:T(8,128)S(1)}, f32[256,128]{1,0:T(8,128)S(1)}, f32[64,128]{1,0:T(8,128)S(1)}, f32[64,128]{1,0:T(8,128)S(1)}, f32[64,128]{1,0:T(8,128)S(1)}, /*index=5*/f32[64,128]{1,0:T(8,128)S(1)}) custom-call(f32[448,128]{1,0:T(8,128)S(1)} %bitcast.25, s32[128,128]{1,0:T(8,128)S(1)} %get-tuple-element.33.pair_ref, f32[64,128]{1,0:T(8,128)} %bitcast.36, ...), custom_call_target="tpu_custom_call" | custom-call | flops 4000000 | bytes 262144 | tf_op jit(solution)/shard_map/image/pallas_call | solution.py:706
  71.9 21.0 %all_to_all.35 = f32[256,1,128]{2,1,0:T(1,128)S(1)} all-to-all(f32[256,1,128]{2,1,0:T(1,128)S(1)} %bitcast.33), channel_id=1, replica_groups=mesh['group'=32,'pencil'=8] {'group','pencil'}, dimensions={0} | all-to-all | bytes 262144 | tf_op jit(solution)/shard_map/all_to_all | solution.py:580
  92.9 0.8 update.1

commit v4 on v3

--- a/solution.py
+++ b/solution.py
@@ -101,6 +101,45 @@
     return acc[0] + acc[1]
 
 
+def gather_mixed(idx_ref, table_ref, out_ref, flip_ref, high_ref, low_ref, permuted, matched):
+    table_rows = table_ref.shape[0]
+    flipped = table_ref[...].T
+    flip_ref[...] = jnp.concatenate(split_pair(flipped), axis=1)
+    store_digits(idx_ref[...], high_ref, low_ref)
+    row_ids = lax.broadcasted_iota(jnp.int32, (table_rows, LANES), 0).astype(F32).astype(BF16)
+    lane_ids = lax.broadcasted_iota(jnp.int32, (LANES, LANES), 0).astype(F32)
+    step = permuted * 8 + matched
+
+    def block(t, carry):
+        base = t * step
+        second = base + permuted * 8
+        select = []
+        for r in range(matched):
+            high = jnp.broadcast_to(high_ref[pl.ds(second + r, 1), :], (table_rows, LANES))
+            select.append(jnp.where(row_ids == high.astype(BF16), BF16(1), BF16(0)))
+        select = jnp.concatenate(select, axis=1)
+        for sub in range(permuted):
+            start = pl.multiple_of(base + 8 * sub, 8)
+            out_ref[pl.ds(start, 8), :] = gather_rows(
+                idx_ref[pl.ds(start, 8), :], lambda a: table_ref[a : a + 1, :], table_rows
+            )
+        rows = lax.dot_general(
+            flip_ref[...],
+            jnp.concatenate([select, select], axis=0),
+            (((1,), (0,)), ((), ())),
+            preferred_element_type=F32,
+        )
+        picked = []
+        for r in range(matched):
+            low = jnp.broadcast_to(low_ref[pl.ds(second + r, 1), :], (LANES, LANES))
+            own = jnp.where(lane_ids == low, rows[:, r * LANES : (r + 1) * LANES], 0.0)
+            picked.append(jnp.sum(own, axis=0, keepdims=True))
+        out_ref[pl.ds(pl.multiple_of(second, 8), matched), :] = jnp.concatenate(picked, axis=0)
+        return carry
+
+    lax.fori_loop(0, idx_ref.shape[0] // step, block, 0)
+
+
 def store_digits(idx, high_ref, low_ref):
     high_ref[...] = lax.shift_right_arithmetic(idx, 7).astype(F32)
     low_ref[...] = jnp.bitwise_and(idx, LANES - 1).astype(F32)
@@ -156,13 +195,11 @@
 
 def back_kernel(
     pair_hbm, dir_hbm, cells_hbm, prim_hbm, ids_hbm, basis_hbm, values_hbm, coeff_hbm,
-    out_ref, idx_ref, cells_ref, small_ref, bxt_ref, bx_ref, bdt_ref, bd_ref, cst_ref,
-    pair_ref, dir_ref, prim_ref, ids_ref, basis_ref, values_ref, coeff_ref,
+    out_ref, idx_ref, cells_ref, small_ref, basis_ref, values_ref, coeff_ref,
+    pair_ref, dir_ref, prim_ref, ids_ref,
     high_ref, low_ref, piece_ref, acc_ref, sems,
 ):
-    pencil = lax.axis_index("pencil")
-    patch = lax.div(pencil, 2)
-    side = lax.rem(pencil, 2)
+    patch = lax.div(lax.axis_index("pencil"), 2)
     copies = start_copies(
         [
             (pair_hbm, pair_ref),
@@ -177,8 +214,6 @@
         sems,
     )
     half = dir_ref.shape[0]
-    for ref in (bx_ref, bxt_ref, bd_ref, bdt_ref):
-        ref[...] = jnp.zeros(ref.shape, BF16)
     copies[0].wait()
     copies[1].wait()
     for k in range(half):
@@ -203,46 +238,6 @@
     small_ref[...] = jnp.zeros(small_ref.shape, F32)
     small_ref[0:1, :] = spread_lanes(prim_ref[...].astype(F32))
     small_ref[1:2, :] = spread_lanes(ids_ref[...].astype(F32))
-    along_x, along_y, along_z = basis_ref[0], basis_ref[1], basis_ref[2]
-    first = lax.broadcasted_iota(jnp.int32, (64, 64), 0)
-    second = lax.broadcasted_iota(jnp.int32, (64, 64), 1)
-    identity = jnp.where(first == second, 1.0, 0.0)
-    half_x = jnp.where(side == 1, along_x[:, 32:64], along_x[:, 0:32])
-    flipped = full_dot(identity, along_x, ((1,), (1,)))
-    half_flipped = jnp.where(side == 1, flipped[32:64], flipped[0:32])
-    flipped_y = full_dot(identity, along_y, ((1,), (1,)))
-    flipped_z = full_dot(identity, along_z, ((1,), (1,)))
-    store_left(bx_ref, 128, [(0, 0, along_x), (64, 64, half_x)])
-    store_left(bxt_ref, 128, [(0, 0, flipped), (64, 64, half_flipped)])
-    store_left(bd_ref, 256, diagonal(along_z, along_y))
-    store_left(bdt_ref, 256, diagonal(flipped_z, flipped_y))
-
-    def spread(column):
-        return jnp.broadcast_to(column, (64, LANES))
-
-    cst_ref[0] = spread(column_of(along_y[0:1]))
-    cst_ref[1] = spread(column_of(along_y[63:64]))
-    cst_ref[2] = spread(column_of(along_z[0:1]))
-    cst_ref[3] = spread(column_of(along_z[63:64]))
-    lane = lax.broadcasted_iota(jnp.int32, (1, LANES), 1)
-
-    def weight(dim):
-        own = jnp.where(
-            side == 1, coeff_ref[2, pl.ds(patch, 1), :], coeff_ref[0, pl.ds(patch, 1), :]
-        )
-        shared = coeff_ref[1, pl.ds(patch, 1), :]
-        own, shared = (
-            jnp.broadcast_to(value[:, dim : dim + 1], (1, LANES)) for value in (own, shared)
-        )
-        return jnp.where(lane < 64, own, jnp.where(lane < 96, shared, 0.0))
-
-    x_values, y_values, z_values = (values_ref[dim, pl.ds(patch, 1), :] for dim in range(3))
-    half_values = jnp.where(side == 1, x_values[:, 32:64], x_values[:, 0:32])
-    lane_values = jnp.concatenate([x_values, half_values, half_values], axis=1)
-    x_term = jnp.where(lane >= 96, 1.0, weight(0) * lane_values)
-    y_term = weight(1) * spread(column_of(y_values))
-    cst_ref[4] = x_term + y_term
-    cst_ref[5] = weight(2) * spread(column_of(z_values))
 
 
 def load_kernel(
@@ -332,9 +327,55 @@
 
 
 def solve_kernel(
-    recv_ref, bxt_ref, bx_ref, bdt_ref, bd_ref, cst_ref, out_ref, fwd_ref, d0_ref, d1_ref,
-    slab_ref, high_ref, low_ref, piece_ref,
+    recv_ref, basis_ref, values_ref, coeff_ref, out_ref, bxt_ref, bx_ref, bdt_ref, bd_ref, cst_ref,
+    fwd_ref, d0_ref, d1_ref, slab_ref, high_ref, low_ref, piece_ref,
 ):
+    pencil = lax.axis_index("pencil")
+    patch = lax.div(pencil, 2)
+    side = lax.rem(pencil, 2)
+    for ref in (bx_ref, bxt_ref, bd_ref, bdt_ref):
+        ref[...] = jnp.zeros(ref.shape, BF16)
+    along_x, along_y, along_z = basis_ref[0], basis_ref[1], basis_ref[2]
+    first = lax.broadcasted_iota(jnp.int32, (64, 64), 0)
+    second = lax.broadcasted_iota(jnp.int32, (64, 64), 1)
+    identity = jnp.where(first == second, 1.0, 0.0)
+    half_x = jnp.where(side == 1, along_x[:, 32:64], along_x[:, 0:32])
+    flipped = full_dot(identity, along_x, ((1,), (1,)))
+    half_flipped = jnp.where(side == 1, flipped[32:64], flipped[0:32])
+    flipped_y = full_dot(identity, along_y, ((1,), (1,)))
+    flipped_z = full_dot(identity, along_z, ((1,), (1,)))
+    store_left(bx_ref, 128, [(0, 0, along_x), (64, 64, half_x)])
+    store_left(bxt_ref, 128, [(0, 0, flipped), (64, 64, half_flipped)])
+    store_left(bd_ref, 256, diagonal(along_z, along_y))
+    store_left(bdt_ref, 256, diagonal(flipped_z, flipped_y))
+
+    def spread(column):
+        return jnp.broadcast_to(column, (64, LANES))
+
+    cst_ref[0] = spread(column_of(along_y[0:1]))
+    cst_ref[1] = spread(column_of(along_y[63:64]))
+    cst_ref[2] = spread(column_of(along_z[0:1]))
+    cst_ref[3] = spread(column_of(along_z[63:64]))
+    lane = lax.broadcasted_iota(jnp.int32, (1, LANES), 1)
+
+    def weight(dim):
+        own = jnp.where(
+            side == 1, coeff_ref[2, pl.ds(patch, 1), :], coeff_ref[0, pl.ds(patch, 1), :]
+        )
+        shared = coeff_ref[1, pl.ds(patch, 1), :]
+        own, shared = (
+            jnp.broadcast_to(value[:, dim : dim + 1], (1, LANES)) for value in (own, shared)
+        )
+        return jnp.where(lane < 64, own, jnp.where(lane < 96, shared, 0.0))
+
+    x_values, y_values, z_values = (values_ref[dim, pl.ds(patch, 1), :] for dim in range(3))
+    half_values = jnp.where(side == 1, x_values[:, 32:64], x_values[:, 0:32])
+    lane_values = jnp.concatenate([x_values, half_values, half_values], axis=1)
+    x_term = jnp.where(lane >= 96, 1.0, weight(0) * lane_values)
+    y_term = weight(1) * spread(column_of(y_values))
+    cst_ref[4] = x_term + y_term
+    cst_ref[5] = weight(2) * spread(column_of(z_values))
+
     sources = recv_ref.shape[0] // LOAD_ROWS
     load = jnp.concatenate(
         [
@@ -416,37 +457,31 @@
 
 def pick_kernel(
     recv_ref, idx_ref, small_ref, inv_hbm, out_ref, table_ref, pick_ref, inv_ref, mid_ref,
-    lift_ref, sem,
+    lift_ref, flip_ref, high_ref, low_ref, sem,
 ):
     copy = pltpu.make_async_copy(inv_hbm, inv_ref, sem)
     copy.start()
     sources = recv_ref.shape[0] // SLAB_ROWS
 
     def block_of(src, start):
-        return recv_ref[SLAB_ROWS * src + start : SLAB_ROWS * src + start + 8, :]
+        return recv_ref[pl.ds(SLAB_ROWS * src + start, 8), :]
 
     coarse = block_of(0, 32)
     for src in range(1, sources):
         coarse = coarse + block_of(src, 32)
-    for p in range(sources // 2):
+
+    def build(p, carry):
         for half in range(2):
-            start = p * 48 + half * 24
-            table_ref[start : start + 8, :] = block_of(2 * p, 16 * half)
-            table_ref[start + 8 : start + 16, :] = block_of(2 * p, 16 * half + 8) + block_of(
+            start = pl.multiple_of(p * 48 + half * 24, 8)
+            table_ref[pl.ds(start, 8), :] = block_of(2 * p, 16 * half)
+            table_ref[pl.ds(start + 8, 8), :] = block_of(2 * p, 16 * half + 8) + block_of(
                 2 * p + 1, 16 * half + 8
             )
-            table_ref[start + 16 : start + 24, :] = block_of(2 * p + 1, 16 * half)
-    table_rows = table_ref.shape[0]
-
-    def block(t, carry):
-        for sub in range(4):
-            start = pl.multiple_of(t * 32 + sub * 8, 8)
-            pick_ref[pl.ds(start, 8), :] = gather_rows(
-                idx_ref[pl.ds(start, 8), :], lambda a: table_ref[a : a + 1, :], table_rows
-            )
+            table_ref[pl.ds(start + 16, 8), :] = block_of(2 * p + 1, 16 * half)
         return carry
 
-    lax.fori_loop(0, 4, block, 0)
+    lax.fori_loop(0, sources // 2, build, 0)
+    gather_mixed(idx_ref, table_ref, pick_ref, flip_ref, high_ref, low_ref, 7, 72)
     mid_ref[...] = coarse
     copy.wait()
     coarse_rows = [jnp.broadcast_to(mid_ref[q : q + 1, :], (LANES, LANES)) for q in range(8)]
@@ -471,7 +506,8 @@
 def image_kernel(
     own_ref, pair_ref, dir_hbm, res_hbm, scale_hbm, iterate_hbm,
     image_ref, sums_ref, dir_ref, res_ref, scale_ref, iterate_ref,
-    lift_ref, high_ref, low_ref, piece_ref, corr_ref, table_ref, sems,
+    lift_ref, high_ref, low_ref, piece_ref, corr_ref, table_ref, flip_ref, pick_ref, wide_high_ref,
+    wide_low_ref, sems,
 ):
     copies = start_copies(
         [
@@ -516,37 +552,21 @@
         table_ref[4 * h : 4 * h + 4, :] = (
             own_ref[start : start + 4, :] + corr_ref[4 * h : 4 * h + 4, :]
         )
+    gather_mixed(pair_ref, table_ref, pick_ref, flip_ref, wide_high_ref, wide_low_ref, 4, 32)
     for copy in copies:
         copy.wait()
-
     half = dir_ref.shape[0]
-    table_rows = 4 * groups
-
-    def block(t, sums):
-        sums = list(sums)
-        for sub in range(2):
-            start = pl.multiple_of(t * 16 + sub * 8, 8)
-            plus, minus = (
-                gather_rows(
-                    pair_ref[pl.ds(base + start, 8), :],
-                    lambda a: table_ref[a : a + 1, :],
-                    table_rows,
-                )
-                for base in (0, half)
-            )
-            image = plus - minus
-            image_ref[pl.ds(start, 8), :] = image
-            res = res_ref[pl.ds(start, 8), :]
-            scaled = scale_ref[pl.ds(start, 8), :]
-            scaled_res = res * scaled
-            sums[0] = sums[0] + scaled_res * res
-            sums[1] = sums[1] + dir_ref[pl.ds(start, 8), :] * image
-            sums[2] = sums[2] + scaled_res * image
-            sums[3] = sums[3] + (scaled * image) * image
-        return tuple(sums)
-
-    zero = jnp.zeros((8, LANES), F32)
-    sums = lax.fori_loop(0, half // 16, block, (zero, zero, zero, zero))
+    sums = [jnp.zeros((8, LANES), F32) for _ in range(4)]
+    for start in range(0, half, 8):
+        rows = slice(start, start + 8)
+        image = pick_ref[rows, :] - pick_ref[half + start : half + start + 8, :]
+        image_ref[rows, :] = image
+        scaled = scale_ref[rows, :]
+        scaled_res = res_ref[rows, :] * scaled
+        sums[0] = sums[0] + scaled_res * res_ref[rows, :]
+        sums[1] = sums[1] + dir_ref[rows, :] * image
+        sums[2] = sums[2] + scaled_res * image
+        sums[3] = sums[3] + (scaled * image) * image
     lane = lax.broadcasted_iota(jnp.int32, (8, LANES), 1)
     packed_sums = jnp.zeros((8, LANES), F32)
     for n, part in enumerate(sums):
@@ -633,18 +653,16 @@
         eigen_values.transpose(1, 0, 2),
         elastic_coef.transpose(1, 0, 2),
     )
-    back, pair_rows, cells, primals, *constants = call(
+    back, pair_rows, cells, primals, *patch_data = call(
         back_kernel,
         (
             f32(128, LANES),
             i32(128, LANES),
             i32(128, LANES),
             f32(8, LANES),
-            jax.ShapeDtypeStruct((128, 384), BF16),
-            jax.ShapeDtypeStruct((128, 384), BF16),
-            jax.ShapeDtypeStruct((256, 768), BF16),
-            jax.ShapeDtypeStruct((256, 768), BF16),
-            f32(6, 64, LANES),
+            f32(3, 64, 64),
+            f32(3, 4, 64),
+            f32(3, 4, 3),
         ),
         [HBM] * len(sources),
         "back",
@@ -653,9 +671,6 @@
             pltpu.VMEM((64, LANES), F32),
             pltpu.VMEM((1, 32), jnp.int32),
             pltpu.VMEM((1, 32), jnp.int32),
-            pltpu.VMEM((3, 64, 64), F32),
-            pltpu.VMEM((3, 4, 64), F32),
-            pltpu.VMEM((3, 4, 3), F32),
         ]
         + digits
         + [pieces, pltpu.VMEM((WIDE, LANES), F32), pltpu.SemaphoreType.DMA((len(sources),))],
@@ -674,16 +689,21 @@
     partial = call(
         solve_kernel,
         f32(pencils * SLAB_ROWS, LANES),
-        [VMEM] * 6,
+        [VMEM] * 4,
         "solve",
         [
+            pltpu.VMEM((128, 384), BF16),
+            pltpu.VMEM((128, 384), BF16),
+            pltpu.VMEM((256, 768), BF16),
+            pltpu.VMEM((256, 768), BF16),
+            pltpu.VMEM((6, 64, LANES), F32),
             pltpu.VMEM((256, LANES), F32),
             pltpu.VMEM((64, 8, LANES), F32),
             pltpu.VMEM((64, 8, LANES), F32),
             pltpu.VMEM((128, 256), F32),
         ]
         + small,
-    )(columns.reshape(pencils * LOAD_ROWS, LANES), *constants)
+    )(columns.reshape(pencils * LOAD_ROWS, LANES), *patch_data)
     slabs = exchange(partial.reshape(pencils, 1, SLAB_ROWS * LANES), "pencil")
 
     picked = call(
@@ -697,6 +717,10 @@
             pltpu.VMEM((1024, 1024), F32),
             pltpu.VMEM((8, LANES), F32),
             pltpu.VMEM((8, LANES), F32),
+            pltpu.VMEM((LANES, 384), BF16),
+        ]
+        + digits
+        + [
             pltpu.SemaphoreType.DMA,
         ],
     )(slabs.reshape(pencils * SLAB_ROWS, LANES), slots, primals, resident(coarse_inverse))
@@ -713,8 +737,11 @@
         + [
             pltpu.VMEM((128, LANES), F32),
             pltpu.VMEM((128, LANES), F32),
-            pltpu.SemaphoreType.DMA((4,)),
-        ],
+            pltpu.VMEM((LANES, 256), BF16),
+            pltpu.VMEM((128, LANES), F32),
+        ]
+        + digits
+        + [pltpu.SemaphoreType.DMA((4,))],
     )(
         owner.reshape(groups * OWNER_ROWS, LANES),
         pair_rows,

time: 94.1 us -> 91.3 us (0.970)
  Pallas kernels: 18.5 us -> 15.8 us
    pallas_call x1, Pallas kernels: 4.08 us -> 2.69 us  [body(): call(pick_kernel, f32(groups * OWNER_ROWS, LANES), [VMEM, VMEM, VMEM, HBM...]
    pallas_call x1, Pallas kernels: 3.45 us -> 2.18 us  [body(): call(image_kernel, (shape, f32(groups * pencils, LANES), shape, shape, sh...]
where the time goes in v4:
time: 91.3 us; the launch traced here: 91 us
  blocking collectives  74.5 us (82%)
  Pallas kernels  15.8 us (17%)
    all_to_all x5, blocking collectives, exchange(): return lax.all_to_all(array, axis, split_axis=0, concat_axis=0, tiled=True)  74.5 us
    pallas_call x1, Pallas kernels, body(): call(back_kernel, (f32(128, LANES), i32(128, LANES), i32(128, LANES), f32...  3.72 us
    pallas_call x1, Pallas kernels, body(): call(solve_kernel, f32(pencils * SLAB_ROWS, LANES), [VMEM] * 4, 'solve',...  3.51 us
    pallas_call x1, Pallas kernels, body(): call(load_kernel, (f32(pencils * LOAD_ROWS, LANES), i32(128, LANES)), [VM...  2.95 us
    pallas_call x1, Pallas kernels, body(): call(pick_kernel, f32(groups * OWNER_ROWS, LANES), [VMEM, VMEM, VMEM, HBM...  2.69 us
    pallas_call x1, Pallas kernels, body(): call(image_kernel, (shape, f32(groups * pencils, LANES), shape, shape, sh...  2.18 us

profile of v4, /device:TPU:1, one launch (start us, length us, event | category | flops | bytes accessed | tf_op | source)
XLA Modules:
  0.0 91.0 jit_solution(8249404556554297123)
XLA Ops:
  0.6 3.7 %back.1 = (f32[128,128]{1,0:T(8,128)S(1)}, s32[128,128]{1,0:T(8,128)S(1)}, s32[128,128]{1,0:T(8,128)S(1)}, f32[8,128]{1,0:T(8,128)S(1)}, f32[3,64,64]{2,1,0:T(8,...) custom-call(s32[2,8192]{1,0:T(2,128)} %bitcast.37, f32[64,128]{1,0:T(8,128)} %bitcast.35, s32[128,128]{1,0:T(8,128)} %bitcast.38, ...), custom_call_target="tpu_custom_call" | custom-call | flops 4000000 | bytes 262144 | tf_op jit(solution)/shard_map/back/pallas_call | solution.py:656
  4.4 20.7 %all_to_all.31 = f32[32,4,128]{2,1,0:T(4,128)S(1)} all-to-all(f32[32,4,128]{2,1,0:T(4,128)S(1)} %bitcast.34), channel_id=1, replica_groups=mesh['group'=32,'pencil'=8] {'group'}, dimensions={0} | all-to-all | bytes 131072 | tf_op jit(solution)/shard_map/all_to_all | solution.py:600
  25.0 2.9 %load.1 = (f32[272,128]{1,0:T(8,128)S(1)}, s32[128,128]{1,0:T(8,128)S(1)}) custom-call(f32[128,128]{1,0:T(8,128)S(1)} %bitcast.31, s32[128,128]{1,0:T(8,128)S(1)} %get-tuple-element.22.pos_ref, f32[8,128]{1,0:T(8,128)S(1)} %get-tuple-element.23.small_ref), custom_call_target="tpu_custom_call" | custom-call | flops 4000000 | bytes 262144 | tf_op jit(solution)/shard_map/load/pallas_call | solution.py:680
  28.0 11.5 %all_to_all.32 = f32[8,1,4352]{2,1,0:T(1,128)S(1)} all-to-all(f32[8,1,4352]{2,1,0:T(1,128)S(1)} %bitcast.32), channel_id=1, replica_groups=mesh['group'=32,'pencil'=8] {'pencil'}, dimensions={0} | all-to-all | bytes 278528 | tf_op jit(solution)/shard_map/all_to_all | solution.py:600
  39.5 3.5 %solve.1 = f32[320,128]{1,0:T(8,128)S(1)} custom-call(f32[272,128]{1,0:T(8,128)S(1)} %bitcast.29, f32[3,64,64]{2,1,0:T(8,128)S(1)} %get-tuple-element.25.basis_ref, f32[3,4,64]{2,1,0:T(4,128)S(1)} %get-tuple-element.26.values_ref, f32[3,4,3]{2,1,0:T(4,128)S(1)} %get-tuple-element.27.coeff_ref), custom_call_target="tpu_custom_call" | custom-call | flops 4000000 | bytes 262144 | tf_op jit(solution)/shard_map/solve/pallas_call | solution.py:689
  43.0 8.8 %all_to_all.33 = f32[8,1,5120]{2,1,0:T(1,128)S(1)} all-to-all(f32[8,1,5120]{2,1,0:T(1,128)S(1)} %bitcast.27), channel_id=1, replica_groups=mesh['group'=32,'pencil'=8] {'pencil'}, dimensions={0} | all-to-all | bytes 327680 | tf_op jit(solution)/shard_map/all_to_all | solution.py:600
  51.9 2.7 %pick.1 = f32[448,128]{1,0:T(8,128)S(1)} custom-call(f32[320,128]{1,0:T(8,128)S(1)} %bitcast.28, s32[128,128]{1,0:T(8,128)S(1)} %get-tuple-element.28.idx_ref, f32[8,128]{1,0:T(8,128)S(1)} %get-tuple-element.23.small_ref, f32[1024,1024]{1,0:T(8,128)} %inv_hbm.1), custom_call_target="tpu_custom_call" | custom-call | flops 4000000 | bytes 262144 | tf_op jit(solution)/shard_map/pick/pallas_call | solution.py:709
  54.6 12.5 %all_to_all.34 = f32[32,1,1792]{2,1,0:T(1,128)S(1)} all-to-all(f32[32,1,1792]{2,1,0:T(1,128)S(1)} %bitcast.26), channel_id=1, replica_groups=mesh['group'=32,'pencil'=8] {'group'}, dimensions={0} | all-to-all | bytes 458752 | tf_op jit(solution)/shard_map/all_to_all | solution.py:600
  67.1 2.2 %image.1 = (f32[64,128]{1,0:T(8,128)S(1)}, f32[256,128]{1,0:T(8,128)S(1)}, f32[64,128]{1,0:T(8,128)S(1)}, f32[64,128]{1,0:T(8,128)S(1)}, f32[64,128]{1,0:T(8,128)S(1)}, /*index=5*/f32[64,128]{1,0:T(8,128)S(1)}) custom-call(f32[448,128]{1,0:T(8,128)S(1)} %bitcast.25, s32[128,128]{1,0:T(8,128)S(1)} %get-tuple-element.29.pair_ref, f32[64,128]{1,0:T(8,128)} %bitcast.36, ...), custom_call_target="tpu_custom_call" | custom-call | flops 4000000 | bytes 262144 | tf_op jit(solution)/shard_map/image/pallas_call | solution.py:730
  69.3 21.0 %all_to_all.35 = f32[256,1,128]{2,1,0:T(1,128)S(1)} all-to-all(f32[256,1,128]{2,1,0:T(1,128)S(1)} %bitcast.33), channel_id=1, replica_groups=mesh['group'=32,'pencil'=8] {'group','pencil'}, dimensions={0} | all-to-all | bytes 262144 | tf_op jit(solution)/shard_map/all_to_all | solution.py:600
  90.3 0.8 update.1

commit v5 on v4

--- a/solution.py
+++ b/solution.py
@@ -8,7 +8,6 @@
 LANES = 128
 BF16 = jnp.bfloat16
 F32 = jnp.float32
-HIGHEST = lax.Precision.HIGHEST
 VMEM = pl.BlockSpec(memory_space=pltpu.VMEM)
 
 
@@ -73,7 +72,11 @@
         )
         return acc + pair_dot(right, left)
 
-    acc = lax.fori_loop(0, total // chunk, step, jnp.zeros((2 * LANES, rows), F32))
+    acc = jnp.zeros((2 * LANES, rows), F32)
+    if total == chunk:
+        acc = step(0, acc)
+    else:
+        acc = lax.fori_loop(0, total // chunk, step, acc)
     return (acc[:LANES] + acc[LANES:]).T
 
 
@@ -176,7 +179,7 @@
     return jnp.concatenate([row] * 4, axis=1)
 
 
-CHUNK = 64
+CHUNK = 128
 WIDE = 192
 LOAD_ROWS = 34
 SLAB_ROWS = 40
@@ -284,13 +287,6 @@
         out_ref[base + 33 : base + 34, :] = ids
 
 
-def full_dot(left, right, contract):
-    return lax.dot_general(
-        left, right, ((contract[0], contract[1]), ((), ())), precision=HIGHEST,
-        preferred_element_type=F32,
-    )
-
-
 def split_pair(value):
     high = value.astype(BF16)
     return high, (value - high.astype(F32)).astype(BF16)
@@ -336,14 +332,11 @@
     for ref in (bx_ref, bxt_ref, bd_ref, bdt_ref):
         ref[...] = jnp.zeros(ref.shape, BF16)
     along_x, along_y, along_z = basis_ref[0], basis_ref[1], basis_ref[2]
-    first = lax.broadcasted_iota(jnp.int32, (64, 64), 0)
-    second = lax.broadcasted_iota(jnp.int32, (64, 64), 1)
-    identity = jnp.where(first == second, 1.0, 0.0)
     half_x = jnp.where(side == 1, along_x[:, 32:64], along_x[:, 0:32])
-    flipped = full_dot(identity, along_x, ((1,), (1,)))
+    flipped = along_x.T
     half_flipped = jnp.where(side == 1, flipped[32:64], flipped[0:32])
-    flipped_y = full_dot(identity, along_y, ((1,), (1,)))
-    flipped_z = full_dot(identity, along_z, ((1,), (1,)))
+    flipped_y = along_y.T
+    flipped_z = along_z.T
     store_left(bx_ref, 128, [(0, 0, along_x), (64, 64, half_x)])
     store_left(bxt_ref, 128, [(0, 0, flipped), (64, 64, half_flipped)])
     store_left(bd_ref, 256, diagonal(along_z, along_y))
@@ -416,7 +409,7 @@
         return top + y_first * scaled, bottom + y_last * scaled
 
     zero = jnp.zeros((64, LANES), F32)
-    top, bottom = lax.fori_loop(0, 64, step, (zero, zero), unroll=4)
+    top, bottom = lax.fori_loop(0, 64, step, (zero, zero), unroll=8)
     edges = jnp.concatenate(
         [top, jnp.sum(d0_ref[...], axis=1), jnp.sum(d1_ref[...], axis=1), bottom], axis=0
     )

time: 91.3 us -> 90.2 us (0.988)
  Pallas kernels: 15.8 us -> 14.7 us
where the time goes in v5:
time: 90.2 us; the launch traced here: 89.9 us
  blocking collectives  74.6 us (83%)
  Pallas kernels  14.7 us (16%)
    all_to_all x5, blocking collectives, exchange(): return lax.all_to_all(array, axis, split_axis=0, concat_axis=0, tiled=True)  74.6 us
    pallas_call x1, Pallas kernels, body(): call(back_kernel, (f32(128, LANES), i32(128, LANES), i32(128, LANES), f32...  3.42 us
    pallas_call x1, Pallas kernels, body(): call(solve_kernel, f32(pencils * SLAB_ROWS, LANES), [VMEM] * 4, 'solve',...  3.14 us
    pallas_call x1, Pallas kernels, body(): call(pick_kernel, f32(groups * OWNER_ROWS, LANES), [VMEM, VMEM, VMEM, HBM...  2.69 us
    pallas_call x1, Pallas kernels, body(): call(load_kernel, (f32(pencils * LOAD_ROWS, LANES), i32(128, LANES)), [VM...  2.48 us
    pallas_call x1, Pallas kernels, body(): call(image_kernel, (shape, f32(groups * pencils, LANES), shape, shape, sh...  2.18 us

profile of v5, /device:TPU:1, one launch (start us, length us, event | category | flops | bytes accessed | tf_op | source)
XLA Modules:
  0.0 89.9 jit_solution(7531049018997561975)
XLA Ops:
  0.6 3.4 %back.1 = (f32[128,128]{1,0:T(8,128)S(1)}, s32[128,128]{1,0:T(8,128)S(1)}, s32[128,128]{1,0:T(8,128)S(1)}, f32[8,128]{1,0:T(8,128)S(1)}, f32[3,64,64]{2,1,0:T(8,...) custom-call(s32[2,8192]{1,0:T(2,128)} %bitcast.37, f32[64,128]{1,0:T(8,128)} %bitcast.35, s32[128,128]{1,0:T(8,128)} %bitcast.38, ...), custom_call_target="tpu_custom_call" | custom-call | flops 4000000 | bytes 262144 | tf_op jit(solution)/shard_map/back/pallas_call | solution.py:649
  4.1 20.7 %all_to_all.31 = f32[32,4,128]{2,1,0:T(4,128)S(1)} all-to-all(f32[32,4,128]{2,1,0:T(4,128)S(1)} %bitcast.34), channel_id=1, replica_groups=mesh['group'=32,'pencil'=8] {'group'}, dimensions={0} | all-to-all | bytes 131072 | tf_op jit(solution)/shard_map/all_to_all | solution.py:593
  24.7 2.5 %load.1 = (f32[272,128]{1,0:T(8,128)S(1)}, s32[128,128]{1,0:T(8,128)S(1)}) custom-call(f32[128,128]{1,0:T(8,128)S(1)} %bitcast.31, s32[128,128]{1,0:T(8,128)S(1)} %get-tuple-element.22.pos_ref, f32[8,128]{1,0:T(8,128)S(1)} %get-tuple-element.23.small_ref), custom_call_target="tpu_custom_call" | custom-call | flops 4000000 | bytes 262144 | tf_op jit(solution)/shard_map/load/pallas_call | solution.py:673
  27.2 11.5 %all_to_all.32 = f32[8,1,4352]{2,1,0:T(1,128)S(1)} all-to-all(f32[8,1,4352]{2,1,0:T(1,128)S(1)} %bitcast.32), channel_id=1, replica_groups=mesh['group'=32,'pencil'=8] {'pencil'}, dimensions={0} | all-to-all | bytes 278528 | tf_op jit(solution)/shard_map/all_to_all | solution.py:593
  38.8 3.1 %solve.1 = f32[320,128]{1,0:T(8,128)S(1)} custom-call(f32[272,128]{1,0:T(8,128)S(1)} %bitcast.29, f32[3,64,64]{2,1,0:T(8,128)S(1)} %get-tuple-element.25.basis_ref, f32[3,4,64]{2,1,0:T(4,128)S(1)} %get-tuple-element.26.values_ref, f32[3,4,3]{2,1,0:T(4,128)S(1)} %get-tuple-element.27.coeff_ref), custom_call_target="tpu_custom_call" | custom-call | flops 4000000 | bytes 262144 | tf_op jit(solution)/shard_map/solve/pallas_call | solution.py:682
  41.9 8.9 %all_to_all.33 = f32[8,1,5120]{2,1,0:T(1,128)S(1)} all-to-all(f32[8,1,5120]{2,1,0:T(1,128)S(1)} %bitcast.27), channel_id=1, replica_groups=mesh['group'=32,'pencil'=8] {'pencil'}, dimensions={0} | all-to-all | bytes 327680 | tf_op jit(solution)/shard_map/all_to_all | solution.py:593
  50.8 2.7 %pick.1 = f32[448,128]{1,0:T(8,128)S(1)} custom-call(f32[320,128]{1,0:T(8,128)S(1)} %bitcast.28, s32[128,128]{1,0:T(8,128)S(1)} %get-tuple-element.28.idx_ref, f32[8,128]{1,0:T(8,128)S(1)} %get-tuple-element.23.small_ref, f32[1024,1024]{1,0:T(8,128)} %inv_hbm.1), custom_call_target="tpu_custom_call" | custom-call | flops 4000000 | bytes 262144 | tf_op jit(solution)/shard_map/pick/pallas_call | solution.py:702
  53.5 12.5 %all_to_all.34 = f32[32,1,1792]{2,1,0:T(1,128)S(1)} all-to-all(f32[32,1,1792]{2,1,0:T(1,128)S(1)} %bitcast.26), channel_id=1, replica_groups=mesh['group'=32,'pencil'=8] {'group'}, dimensions={0} | all-to-all | bytes 458752 | tf_op jit(solution)/shard_map/all_to_all | solution.py:593
  66.0 2.2 %image.1 = (f32[64,128]{1,0:T(8,128)S(1)}, f32[256,128]{1,0:T(8,128)S(1)}, f32[64,128]{1,0:T(8,128)S(1)}, f32[64,128]{1,0:T(8,128)S(1)}, f32[64,128]{1,0:T(8,128)S(1)}, /*index=5*/f32[64,128]{1,0:T(8,128)S(1)}) custom-call(f32[448,128]{1,0:T(8,128)S(1)} %bitcast.25, s32[128,128]{1,0:T(8,128)S(1)} %get-tuple-element.29.pair_ref, f32[64,128]{1,0:T(8,128)} %bitcast.36, ...), custom_call_target="tpu_custom_call" | custom-call | flops 4000000 | bytes 262144 | tf_op jit(solution)/shard_map/image/pallas_call | solution.py:723
  68.2 21.0 %all_to_all.35 = f32[256,1,128]{2,1,0:T(1,128)S(1)} all-to-all(f32[256,1,128]{2,1,0:T(1,128)S(1)} %bitcast.33), channel_id=1, replica_groups=mesh['group'=32,'pencil'=8] {'group','pencil'}, dimensions={0} | all-to-all | bytes 262144 | tf_op jit(solution)/shard_map/all_to_all | solution.py:593
  89.2 0.8 update.1

commit v6 on v5

--- a/solution.py
+++ b/solution.py
@@ -545,7 +545,7 @@
         table_ref[4 * h : 4 * h + 4, :] = (
             own_ref[start : start + 4, :] + corr_ref[4 * h : 4 * h + 4, :]
         )
-    gather_mixed(pair_ref, table_ref, pick_ref, flip_ref, wide_high_ref, wide_low_ref, 4, 32)
+    gather_mixed(pair_ref, table_ref, pick_ref, flip_ref, wide_high_ref, wide_low_ref, 3, 40)
     for copy in copies:
         copy.wait()
     half = dir_ref.shape[0]

time: 90.2 us -> 90.1 us (level)
  no operation moved by 1% of the time
where the time goes in v6:
time: 90.1 us; the launch traced here: 89.8 us
  blocking collectives  74.6 us (83%)
  Pallas kernels  14.5 us (16%)
    all_to_all x5, blocking collectives, exchange(): return lax.all_to_all(array, axis, split_axis=0, concat_axis=0, tiled=True)  74.6 us
    pallas_call x1, Pallas kernels, body(): call(back_kernel, (f32(128, LANES), i32(128, LANES), i32(128, LANES), f32...  3.42 us
    pallas_call x1, Pallas kernels, body(): call(solve_kernel, f32(pencils * SLAB_ROWS, LANES), [VMEM] * 4, 'solve',...  3.14 us
    pallas_call x1, Pallas kernels, body(): call(pick_kernel, f32(groups * OWNER_ROWS, LANES), [VMEM, VMEM, VMEM, HBM...  2.69 us
    pallas_call x1, Pallas kernels, body(): call(load_kernel, (f32(pencils * LOAD_ROWS, LANES), i32(128, LANES)), [VM...  2.48 us
    pallas_call x1, Pallas kernels, body(): call(image_kernel, (shape, f32(groups * pencils, LANES), shape, shape, sh...  2.02 us

profile of v6, /device:TPU:1, one launch (start us, length us, event | category | flops | bytes accessed | tf_op | source)
XLA Modules:
  0.0 89.8 jit_solution(14359843753264440438)
XLA Ops:
  0.6 3.4 %back.1 = (f32[128,128]{1,0:T(8,128)S(1)}, s32[128,128]{1,0:T(8,128)S(1)}, s32[128,128]{1,0:T(8,128)S(1)}, f32[8,128]{1,0:T(8,128)S(1)}, f32[3,64,64]{2,1,0:T(8,...) custom-call(s32[2,8192]{1,0:T(2,128)} %bitcast.37, f32[64,128]{1,0:T(8,128)} %bitcast.35, s32[128,128]{1,0:T(8,128)} %bitcast.38, ...), custom_call_target="tpu_custom_call" | custom-call | flops 4000000 | bytes 262144 | tf_op jit(solution)/shard_map/back/pallas_call | solution.py:649
  4.1 20.7 %all_to_all.31 = f32[32,4,128]{2,1,0:T(4,128)S(1)} all-to-all(f32[32,4,128]{2,1,0:T(4,128)S(1)} %bitcast.34), channel_id=1, replica_groups=mesh['group'=32,'pencil'=8] {'group'}, dimensions={0} | all-to-all | bytes 131072 | tf_op jit(solution)/shard_map/all_to_all | solution.py:593
  24.7 2.5 %load.1 = (f32[272,128]{1,0:T(8,128)S(1)}, s32[128,128]{1,0:T(8,128)S(1)}) custom-call(f32[128,128]{1,0:T(8,128)S(1)} %bitcast.31, s32[128,128]{1,0:T(8,128)S(1)} %get-tuple-element.22.pos_ref, f32[8,128]{1,0:T(8,128)S(1)} %get-tuple-element.23.small_ref), custom_call_target="tpu_custom_call" | custom-call | flops 4000000 | bytes 262144 | tf_op jit(solution)/shard_map/load/pallas_call | solution.py:673
  27.2 11.5 %all_to_all.32 = f32[8,1,4352]{2,1,0:T(1,128)S(1)} all-to-all(f32[8,1,4352]{2,1,0:T(1,128)S(1)} %bitcast.32), channel_id=1, replica_groups=mesh['group'=32,'pencil'=8] {'pencil'}, dimensions={0} | all-to-all | bytes 278528 | tf_op jit(solution)/shard_map/all_to_all | solution.py:593
  38.8 3.1 %solve.1 = f32[320,128]{1,0:T(8,128)S(1)} custom-call(f32[272,128]{1,0:T(8,128)S(1)} %bitcast.29, f32[3,64,64]{2,1,0:T(8,128)S(1)} %get-tuple-element.25.basis_ref, f32[3,4,64]{2,1,0:T(4,128)S(1)} %get-tuple-element.26.values_ref, f32[3,4,3]{2,1,0:T(4,128)S(1)} %get-tuple-element.27.coeff_ref), custom_call_target="tpu_custom_call" | custom-call | flops 4000000 | bytes 262144 | tf_op jit(solution)/shard_map/solve/pallas_call | solution.py:682
  41.9 8.9 %all_to_all.33 = f32[8,1,5120]{2,1,0:T(1,128)S(1)} all-to-all(f32[8,1,5120]{2,1,0:T(1,128)S(1)} %bitcast.27), channel_id=1, replica_groups=mesh['group'=32,'pencil'=8] {'pencil'}, dimensions={0} | all-to-all | bytes 327680 | tf_op jit(solution)/shard_map/all_to_all | solution.py:593
  50.8 2.7 %pick.1 = f32[448,128]{1,0:T(8,128)S(1)} custom-call(f32[320,128]{1,0:T(8,128)S(1)} %bitcast.28, s32[128,128]{1,0:T(8,128)S(1)} %get-tuple-element.28.idx_ref, f32[8,128]{1,0:T(8,128)S(1)} %get-tuple-element.23.small_ref, f32[1024,1024]{1,0:T(8,128)} %inv_hbm.1), custom_call_target="tpu_custom_call" | custom-call | flops 4000000 | bytes 262144 | tf_op jit(solution)/shard_map/pick/pallas_call | solution.py:702
  53.5 12.5 %all_to_all.34 = f32[32,1,1792]{2,1,0:T(1,128)S(1)} all-to-all(f32[32,1,1792]{2,1,0:T(1,128)S(1)} %bitcast.26), channel_id=1, replica_groups=mesh['group'=32,'pencil'=8] {'group'}, dimensions={0} | all-to-all | bytes 458752 | tf_op jit(solution)/shard_map/all_to_all | solution.py:593
  66.0 2.0 %image.1 = (f32[64,128]{1,0:T(8,128)S(1)}, f32[256,128]{1,0:T(8,128)S(1)}, f32[64,128]{1,0:T(8,128)S(1)}, f32[64,128]{1,0:T(8,128)S(1)}, f32[64,128]{1,0:T(8,128)S(1)}, /*index=5*/f32[64,128]{1,0:T(8,128)S(1)}) custom-call(f32[448,128]{1,0:T(8,128)S(1)} %bitcast.25, s32[128,128]{1,0:T(8,128)S(1)} %get-tuple-element.29.pair_ref, f32[64,128]{1,0:T(8,128)} %bitcast.36, ...), custom_call_target="tpu_custom_call" | custom-call | flops 4000000 | bytes 262144 | tf_op jit(solution)/shard_map/image/pallas_call | solution.py:723
  68.0 21.0 %all_to_all.35 = f32[256,1,128]{2,1,0:T(1,128)S(1)} all-to-all(f32[256,1,128]{2,1,0:T(1,128)S(1)} %bitcast.33), channel_id=1, replica_groups=mesh['group'=32,'pencil'=8] {'group','pencil'}, dimensions={0} | all-to-all | bytes 262144 | tf_op jit(solution)/shard_map/all_to_all | solution.py:593
  89.0 0.8 update.1
